TPU v7x, 32 devices: a whole 2x2x4 slice. The times are simulated.
32 devices in a mesh: dp: 8 (over y, x, core), mp: 4 (over z).
Axes of the slice: x: 2, y: 2, z: 4, core: 2. Of those that a mesh axis runs over, the one named last changes fastest.
Arguments:
- activations: bfloat16 [128, 288, 768], P(('dp', 'mp')), may hold values from -2.5 to 2.5
- cotangent: bfloat16 [128, 288, 768], P(('dp', 'mp')), may hold values from -2.5 to 2.5
- segments: int32 [128, 288], P('dp'), may hold values from 0 to 2, never falling along the last dimension, each value on 1 to 160 neighbouring positions
- triple_weight: bfloat16 [3, 768, 768], P(None, None, 'mp'), may hold values from -0.21875 to 0.21875
- query_value_bias: bfloat16 [2, 12, 64], P(None, 'mp'), may hold values from -1.5 to 1.5
- output_weight: bfloat16 [768, 768], P('mp'), may hold values from -0.875 to 0.875
- expand_weight: bfloat16 [768, 3072], P(None, 'mp'), may hold values from -0.21875 to 0.21875
- expand_bias: bfloat16 [48, 64], P('mp'), may hold values from -1.5 to 1.5
- shrink_weight: bfloat16 [3072, 768], P('mp'), may hold values from -0.109375 to 0.109375
- vector_params: bfloat16 [6, 768], replicated
- triple_master: float32 [3, 768, 768], P(None, 'dp', 'mp'), may hold values from -0.21875 to 0.21875
- triple_first: float32 [3, 768, 768], P(None, 'dp', 'mp'), may hold values from -144 to 144
- triple_second: float32 [3, 768, 768], P(None, 'dp', 'mp'), may hold values from 2211.84 to 8847.36
- query_value_master: float32 [2, 12, 64], P(None, 'mp', 'dp'), may hold values from -1.5 to 1.5
- query_value_first: float32 [2, 12, 64], P(None, 'mp', 'dp'), may hold values from -192 to 192
- query_value_second: float32 [2, 12, 64], P(None, 'mp', 'dp'), may hold values from 3944.448 to 15851.52
- output_master: float32 [768, 768], P('mp', 'dp'), may hold values from -0.875 to 0.875
- output_first: float32 [768, 768], P('mp', 'dp'), may hold values from -57.6 to 57.6
- output_second: float32 [768, 768], P('mp', 'dp'), may hold values from 353.8944 to 1400.832
- expand_master: float32 [768, 3072], P('dp', 'mp'), may hold values from -0.21875 to 0.21875
- expand_first: float32 [768, 3072], P('dp', 'mp'), may hold values from -96 to 96
- expand_second: float32 [768, 3072], P('dp', 'mp'), may hold values from 995.328 to 3944.448
- expand_bias_master: float32 [48, 64], P('mp', 'dp'), may hold values from -1.5 to 1.5
- expand_bias_first: float32 [48, 64], P('mp', 'dp'), may hold values from -96 to 96
- expand_bias_second: float32 [48, 64], P('mp', 'dp'), may hold values from 995.328 to 3944.448
- shrink_master: float32 [3072, 768], P('mp', 'dp'), may hold values from -0.109375 to 0.109375
- shrink_first: float32 [3072, 768], P('mp', 'dp'), may hold values from -192 to 192
- shrink_second: float32 [3072, 768], P('mp', 'dp'), may hold values from 3944.448 to 15851.52
- vector_master: float32 [6, 768], P(None, ('dp', 'mp'))
- vector_first: float32 [6, 768], P(None, ('dp', 'mp')), may hold values from -384 to 384
- vector_second: float32 [6, 768], P(None, ('dp', 'mp')), may hold values from 15851.52 to 62668.8
Outputs:
- block_output: bfloat16 [128, 288, 768], P(('dp', 'mp'))
- input_grad: float32 [128, 288, 768], P(('dp', 'mp'))
- triple_master_new: float32 [3, 768, 768], P(None, 'dp', 'mp')
- triple_first_new: float32 [3, 768, 768], P(None, 'dp', 'mp')
- triple_second_new: float32 [3, 768, 768], P(None, 'dp', 'mp')
- triple_copy: bfloat16 [3, 768, 768], P(None, 'dp', 'mp')
- query_value_master_new: float32 [2, 12, 64], P(None, 'mp', 'dp')
- query_value_first_new: float32 [2, 12, 64], P(None, 'mp', 'dp')
- query_value_second_new: float32 [2, 12, 64], P(None, 'mp', 'dp')
- query_value_copy: bfloat16 [2, 12, 64], P(None, 'mp', 'dp')
- output_master_new: float32 [768, 768], P('mp', 'dp')
- output_first_new: float32 [768, 768], P('mp', 'dp')
- output_second_new: float32 [768, 768], P('mp', 'dp')
- output_copy: bfloat16 [768, 768], P('mp', 'dp')
- expand_master_new: float32 [768, 3072], P('dp', 'mp')
- expand_first_new: float32 [768, 3072], P('dp', 'mp')
- expand_second_new: float32 [768, 3072], P('dp', 'mp')
- expand_copy: bfloat16 [768, 3072], P('dp', 'mp')
- expand_bias_master_new: float32 [48, 64], P('mp', 'dp')
- expand_bias_first_new: float32 [48, 64], P('mp', 'dp')
- expand_bias_second_new: float32 [48, 64], P('mp', 'dp')
- expand_bias_copy: bfloat16 [48, 64], P('mp', 'dp')
- shrink_master_new: float32 [3072, 768], P('mp', 'dp')
- shrink_first_new: float32 [3072, 768], P('mp', 'dp')
- shrink_second_new: float32 [3072, 768], P('mp', 'dp')
- shrink_copy: bfloat16 [3072, 768], P('mp', 'dp')
- vector_master_new: float32 [6, 768], P(None, ('dp', 'mp'))
- vector_first_new: float32 [6, 768], P(None, ('dp', 'mp'))
- vector_second_new: float32 [6, 768], P(None, ('dp', 'mp'))
- vector_copy: bfloat16 [6, 768], P(None, ('dp', 'mp'))
Inputs may be any that keep to these rules, and one draw needn't show every extreme that they name: `segments`: along a row the pair numbers never fall; each pair has 1 to 160 tokens, and each row has one pair of exactly 160.
All inputs are finite; a program needn't handle non-finite values.
Results may differ from a plain program's by a relative error of at most 0.018.
Values may be sent and summed in bfloat16 or wider, within the bound.
A program may use at most 256 MiB of HBM per device.

v0:
```python
import functools

import jax
import jax.numpy as jnp
from jax import lax
from jax.experimental import pallas as pl
from jax.experimental.pallas import tpu as pltpu
from jax.sharding import PartitionSpec as P

D = 768
HEAD = 64
FF = 3072
STEP = 10


NORM_EPS = 1e-05
BETA_ONE = 0.5
BETA_TWO = 0.6
ADAM_EPS = 1e-08
WEIGHT_DECAY = 0.01
MASKED = -1e30
SQRT_HALF = 0.7071067811865476
INV_ROOT_TAU = 0.3989422804014327


def norm_forward(summed, gain, shift):
    centre = summed - jnp.mean(summed, axis=-1, keepdims=True)
    scale = lax.rsqrt(jnp.mean(centre * centre, axis=-1, keepdims=True) + NORM_EPS)
    normed = centre * scale
    return (gain * normed + shift, normed, scale)


def norm_backward(gradient, gain, normed, scale):
    scaled = gradient * gain
    centred = scaled - jnp.mean(scaled, axis=-1, keepdims=True)
    return scale * (centred - normed * jnp.mean(scaled * normed, axis=-1, keepdims=True))


def adam_update(master, first, second, gradient, rate):
    first_new = BETA_ONE * first + (1.0 - BETA_ONE) * gradient
    second_new = BETA_TWO * second + (1.0 - BETA_TWO) * gradient * gradient
    corrected = first_new / (1.0 - BETA_ONE**STEP)
    spread = jnp.sqrt(second_new / (1.0 - BETA_TWO**STEP))
    master_new = master - rate * (corrected / (spread + ADAM_EPS) + WEIGHT_DECAY * master)
    return (master_new, first_new, second_new, master_new.astype(jnp.bfloat16))


MESH = pl.DeviceIdType.MESH
BF = jnp.bfloat16
F32 = jnp.float32
HALF = 48
SLICE = 96
SMALL = 16
VECTORS = 8


def place():
    p, z = lax.axis_index("dp"), lax.axis_index("mp")
    core, xy = p % 2, p // 2
    x, y = xy % 2, xy // 2
    return p, z, core, xy, p + 1 - 2 * core, p + 2 - 4 * x, p + 4 - 8 * y, xy + 1 - 2 * x, xy + 2 - 4 * y


def remote(src, dst, send_sem, recv_sem, p, z):
    return pltpu.make_async_remote_copy(
        src_ref=src, dst_ref=dst, send_sem=send_sem, recv_sem=recv_sem, device_id=(p, z), device_id_type=MESH
    )


def greet(p, z, pc, px, py):
    barrier = pltpu.get_barrier_semaphore()
    for peer in ((pc, z), (px, z), (py, z), (p, (z + 1) % 4), (p, (z + 2) % 4), (p, (z + 3) % 4)):
        pl.semaphore_signal(barrier, inc=1, device_id=peer, device_id_type=MESH)
    pl.semaphore_wait(barrier, 6)


class Gather:
    steps = [(0, 1), (0, 2), (0, 3), (1, 1), (2, 1), (1, 2), (2, 2), (1, 3), (2, 3)]
    sems = [(3,)] + [(3, 3)] * 12 + [(3,)] * 2

    def __init__(self, mats, whole, bias, biases, sems):
        self.mats, self.whole, self.bias, self.biases = mats, whole, bias, biases
        (self.ls, self.zs, self.zr, self.xs, self.xr, self.ys, self.yr, self.as_, self.ar, self.bs, self.br, self.cs,
         self.cr, self.ss, self.sr) = sems
        self.where = place()

    def local(self, m):
        z = self.where[1]
        return pltpu.make_async_copy(self.mats[m - 1], self.whole.at[m, z], self.ls.at[m])

    def small(self, d):
        p, z = self.where[:2]
        return remote(self.bias, self.biases.at[z], self.ss.at[d - 1], self.sr.at[d - 1], p, (z + d) % 4)

    def along_z(self, m, d):
        p, z, core, xy = self.where[:4]
        own = self.whole.at[m, z] if m == 0 else self.mats[m - 1]
        return remote(own.at[xy, core], self.whole.at[m, z, xy, core], self.zs.at[m, d - 1],
                      self.zr.at[m, d - 1], p, (z + d) % 4)

    def plane(self, m, d, block, rows, send_sem, recv_sem, peer):
        z = self.where[1]
        part = self.whole.at[m, (z + 4 - d) % 4, block, self.where[2], rows]
        return remote(part, part, send_sem.at[m, d - 1], recv_sem.at[m, d - 1], peer, z)

    def to_x(self, m, d):
        return self.plane(m, d, self.where[3], slice(None), self.xs, self.xr, self.where[5])

    def to_y(self, m, d):
        return self.plane(m, d, self.where[3], slice(None), self.ys, self.yr, self.where[6])

    def on_to_y(self, m, d):
        return self.plane(m, d, self.where[7], pl.ds(0, HALF), self.as_, self.ar, self.where[6])

    def on_to_x(self, m, d):
        return self.plane(m, d, self.where[8], pl.ds(HALF, HALF), self.bs, self.br, self.where[5])

    def to_core(self, m, d):
        z = self.where[1]
        part = self.whole.at[m, (z + 4 - d) % 4, :, self.where[2]]
        return remote(part, part, self.cs.at[m, d - 1], self.cr.at[m, d - 1], self.where[4], z)

    def begin(self):
        p, z, _, _, pc, px, py = self.where[:7]
        greet(p, z, pc, px, py)
        for d in (1, 2, 3):
            self.along_z(0, d).start()
            self.small(d).start()

    def stage(self, i):
        steps, n = self.steps, len(self.steps)
        if i < n:
            m, d = steps[i]
            self.along_z(m, d).wait_recv()
            if i < 3:
                self.small(d).wait_recv()
            self.to_x(m, d).start()
            self.to_y(m, d).start()
            if m < 2:
                self.along_z(m + 1, d).start()
        if 0 <= i - 1 < n:
            self.to_x(*steps[i - 1]).wait_recv()
            self.to_y(*steps[i - 1]).wait_recv()
            self.on_to_y(*steps[i - 1]).start()
            self.on_to_x(*steps[i - 1]).start()
        if 0 <= i - 2 < n:
            self.on_to_y(*steps[i - 2]).wait_recv()
            self.on_to_x(*steps[i - 2]).wait_recv()
            self.to_core(*steps[i - 2]).start()
        if 0 <= i - 3 < n:
            self.to_core(*steps[i - 3]).wait_recv()

    def finish(self):
        for d in (1, 2, 3):
            self.small(d).wait_send()
        for m, d in self.steps:
            for copy in (self.along_z, self.to_x, self.to_y, self.on_to_y, self.on_to_x, self.to_core):
                copy(m, d).wait_send()


class Scatter:
    steps = [(m, k) for k in range(4) for m in (2, 1)] + [(0, k) for k in range(4)]
    slots = [k + 4 * j for k in range(4) for j in (0, 1)] + list(range(4))
    buffers = [((12, 4, SLICE, D), BF)] + [((12, 2, HALF, D), BF)] * 2 + [((12, HALF, D), BF)] * 2 + [
        ((3, 3, SLICE, D), BF), ((3, 4, SLICE, D), BF), ((6, SMALL, D), F32), ((3, SMALL, D), F32)]
    sems = [(12,)] * 2 + [(12, 2)] * 4 + [(12,)] * 4 + [(3, 3)] * 2 + [(6,)] * 2

    def __init__(self, grads, buffers, sems):
        self.grads = grads
        self.sum, self.rx, self.ry, self.ra, self.rb, self.rz, self.plane, self.rv, self.sv = buffers
        (self.cs, self.cr, self.xs, self.xr, self.ys, self.yr, self.as_, self.ar, self.bs, self.br, self.zs, self.zr,
         self.ss, self.sr) = sems
        self.where = place()

    def to_core(self, i):
        _, z, core, _, pc = self.where[:5]
        return remote(self.grads.at[self.slots[i], :, 1 - core], self.sum.at[i], self.cs.at[i], self.cr.at[i], pc, z)

    def to_x(self, i, t):
        q = (self.where[7], 3 - self.where[3])[t]
        return remote(self.sum.at[i, q, pl.ds(0, HALF)], self.rx.at[i, t], self.xs.at[i, t], self.xr.at[i, t],
                      self.where[5], self.where[1])

    def to_y(self, i, t):
        q = (self.where[8], 3 - self.where[3])[t]
        return remote(self.sum.at[i, q, pl.ds(HALF, HALF)], self.ry.at[i, t], self.ys.at[i, t], self.yr.at[i, t],
                      self.where[6], self.where[1])

    def on_to_y(self, i):
        return remote(self.sum.at[i, self.where[8], pl.ds(0, HALF)], self.ra.at[i], self.as_.at[i], self.ar.at[i],
                      self.where[6], self.where[1])

    def on_to_x(self, i):
        return remote(self.sum.at[i, self.where[7], pl.ds(HALF, HALF)], self.rb.at[i], self.bs.at[i], self.br.at[i],
                      self.where[5], self.where[1])

    def to_owner(self, m, k, d):
        p = self.where[0]
        return remote(self.plane.at[m, k], self.rz.at[m, d - 1], self.zs.at[m, d - 1], self.zr.at[m, d - 1], p, k)

    def along_z(self, m, d):
        return self.to_owner(m, (self.where[1] + d) % 4, d)

    def begin(self):
        p, z, _, _, pc, px, py = self.where[:7]
        greet(p, z, pc, px, py)

    def stage(self, i):
        n = len(self.steps)
        core, xy, xyx, xyy = self.where[2], self.where[3], self.where[7], self.where[8]
        low, high = slice(0, HALF), slice(HALF, SLICE)
        if i < n:
            self.to_core(i).start()
        j = i - 1
        if 0 <= j < n:
            self.to_core(j).wait_recv()

            @pl.loop(0, 4)
            def _(q):
                mine = self.grads[self.slots[j], q, core].astype(F32)
                self.sum[j, q] = (self.sum[j, q].astype(F32) + mine).astype(BF)

            for t in (0, 1):
                self.to_x(j, t).start()
                self.to_y(j, t).start()
        j = i - 2
        if 0 <= j < n:
            for t in (0, 1):
                self.to_x(j, t).wait_recv()
                self.to_y(j, t).wait_recv()
            self.sum[j, xyy, low] = (self.sum[j, xyy, low].astype(F32) + self.rx[j, 1].astype(F32)).astype(BF)
            self.sum[j, xyx, high] = (self.sum[j, xyx, high].astype(F32) + self.ry[j, 1].astype(F32)).astype(BF)
            self.on_to_y(j).start()
            self.on_to_x(j).start()
        j = i - 3
        if 0 <= j < n:
            m, k = self.steps[j]
            self.on_to_y(j).wait_recv()
            self.on_to_x(j).wait_recv()
            self.plane[m, k, low] = (
                self.sum[j, xy, low].astype(F32) + self.rx[j, 0].astype(F32) + self.ra[j].astype(F32)
            ).astype(BF)
            self.plane[m, k, high] = (
                self.sum[j, xy, high].astype(F32) + self.ry[j, 0].astype(F32) + self.rb[j].astype(F32)
            ).astype(BF)
            z = self.where[1]
            pl.when(z != k)(lambda: self.to_owner(m, k, (k + 4 - z) % 4).start())

    def total(self, m):
        for d in (1, 2, 3):
            self.along_z(m, d).wait_recv()
        own = self.plane[m, self.where[1]].astype(F32)
        return own + self.rz[m, 0].astype(F32) + self.rz[m, 1].astype(F32) + self.rz[m, 2].astype(F32)

    def small_to(self, s, src, p, z):
        return remote(src, self.rv.at[s], self.ss.at[s], self.sr.at[s], p, z)

    def small_copy(self, part, c):
        p, z, _, _, pc, px, py = self.where[:7]
        if c == 0:
            return self.small_to(0, part, pc, z)
        if c == 1:
            return self.small_to(1, self.sv.at[0], px, z)
        if c == 2:
            return self.small_to(2, self.sv.at[1], py, z)
        return self.small_to(c, self.sv.at[2], p, (z + c - 2) % 4)

    def small_stage(self, part, i):
        if i == 0:
            self.small_copy(part, 0).start()
        elif i < 4:
            self.small_copy(part, i - 1).wait_recv()
            before = part[...] if i == 1 else self.sv[i - 2]
            self.sv[i - 1] = before + self.rv[i - 1]
            for c in (i,) if i < 3 else (3, 4, 5):
                self.small_copy(part, c).start()
        else:
            for c in (3, 4, 5):
                self.small_copy(part, c).wait_recv()
            return self.sv[2] + self.rv[3] + self.rv[4] + self.rv[5]

    def finish(self, part):
        for c in range(6):
            self.small_copy(part, c).wait_send()
        for i in range(len(self.steps)):
            if self.slots[i] not in self.slots[i + 1 :]:
                self.to_core(i).wait_send()
            self.on_to_y(i).wait_send()
            self.on_to_x(i).wait_send()
            for t in (0, 1):
                self.to_x(i, t).wait_send()
                self.to_y(i, t).wait_send()
        for m in range(3):
            for d in (1, 2, 3):
                self.along_z(m, d).wait_send()


def mm(a, b, dims):
    return lax.dot_general(a, b, (dims, ((), ())), preferred_element_type=jnp.float32)


def pack_weights(triple_weight, output_weight, expand_weight, shrink_weight):
    width = triple_weight.shape[2]
    mixing = jnp.concatenate([triple_weight.transpose(1, 0, 2).reshape(D, 3 * width), output_weight.T], axis=1)
    return mixing, expand_weight, shrink_weight


def pack_biases(query_value_bias, expand_bias):
    pair = query_value_bias.reshape(2, -1)
    none = jnp.zeros_like(pair[0])
    first = jnp.concatenate([pair[0], none, pair[1], none])
    return jnp.concatenate([first[None], expand_bias.reshape(1, -1), jnp.zeros((VECTORS - 2, D), BF)]).astype(F32)


TN = ((0,), (0,))
NT = ((1,), (1,))
NN = ((1,), (0,))
CHUNK = 384
STRIP = 128
TILE = 256
VMEM_MOST = 60 << 20
ATTEND_STAGES = {(0, 1): 1, (0, 3): 2, (1, 1): 4, (2, 0): 5, (2, 3): 6, (3, 2): 7}
FEED_STAGES = {(0, 0): 8, (0, 2): 9, (1, 0): 10, (1, 2): 11}


def tile(n):
    return pl.ds(pl.multiple_of(n * TILE, TILE), TILE)


def strip(s):
    return pl.ds(pl.multiple_of(s * STRIP, STRIP), STRIP)


def forward_kernel(fused, rows, length, *refs):
    n_sem = len(Gather.sems) if fused else 0
    x_in, cot_in, seg_ref, vec_in = refs[:4]
    n_in = 10 if fused else 6
    ins = refs[4:n_in]
    outs = refs[n_in : n_in + 12]
    (whole_out, qkv_out, ctx_out, prob_out, act_out, slope_out, normed_out, rstd_out, ds_out, turned_out, result_out,
     part_out) = outs
    rest = refs[n_in + 12 :]
    gather_sems, rest = rest[:n_sem], rest[n_sem:]
    (whole, bias, biases, joint, vec, x, cot, qkv, ctx, prob, act, slope, mixed, normed, rstd, low, turned,
     result, part, in_sem, w_sem, qkv_sem, ctx_sem, prob_sem, act_sem, slope_sem, end_sem) = rest
    tokens = rows * length
    strips = tokens // STRIP
    heads = D // HEAD // 4
    width = heads * HEAD
    z_own = lax.axis_index("mp")
    x_copy = pltpu.make_async_copy(x_in, x, in_sem.at[0])
    cot_copy = pltpu.make_async_copy(cot_in, cot, in_sem.at[1])
    x_copy.start()
    if fused:
        triple_in, output_in, e_ref, s_ref, qv_ref, eb_ref = ins
        joint_copies = [
            pltpu.make_async_copy(triple_in.at[j], joint.at[pl.ds(j * width, width)], in_sem.at[2 + j]) for j in range(3)
        ] + [pltpu.make_async_copy(output_in, joint.at[pl.ds(3 * width, width)], in_sem.at[5])]
        for copy in joint_copies:
            copy.start()
        gather = Gather((e_ref, s_ref), whole, bias, biases, gather_sems)
        stage = gather.stage
        bias[...] = jnp.zeros_like(bias)
        for h in range(heads):
            for j in (0, 1):
                at = slice(2 * j * width + h * HEAD, 2 * j * width + (h + 1) * HEAD)
                bias[0:1, at] = qv_ref[h, j : j + 1, :].astype(F32)
        for b in range(D // HEAD):
            bias[1:2, b * HEAD : (b + 1) * HEAD] = eb_ref[b : b + 1, :].astype(F32)
        for copy in joint_copies:
            copy.wait()
        for j in (0, 1):
            half = joint[:, j * CHUNK : (j + 1) * CHUNK].T
            whole[0, z_own, 2 * j : 2 * j + 2] = half.reshape(2, 2, SLICE, D)
        gather.begin()
        gather.local(1).start()
        gather.local(2).start()
        own_bias = pltpu.make_async_copy(bias, biases.at[z_own], w_sem.at[0])
        own_bias.start()
        own_bias.wait()
    else:
        copy = pltpu.make_async_copy(ins[0], whole, w_sem.at[0])
        copy.start()
        small = pltpu.make_async_copy(ins[1], biases, w_sem.at[1])
        small.start()
        copy.wait()
        small.wait()
        stage = lambda i: None
    cot_copy.start()
    vec[0:6, :] = vec_in[...].astype(F32)

    def block(i):
        return (z_own + 3 * i) % 4

    def columns(m, z, n):
        return whole[m, z, :, :, :, tile(n)].reshape(D, TILE)

    def turned_copy(slot):
        return pltpu.make_async_copy(turned.at[slot], turned_out.at[slot], end_sem.at[slot])

    def qkv_copy(i):
        return pltpu.make_async_copy(qkv.at[i % 2], qkv_out.at[block(i)], qkv_sem.at[i % 2])

    def ctx_copy(i):
        return pltpu.make_async_copy(ctx.at[i % 2], ctx_out.at[block(i)], ctx_sem.at[i % 2])

    def prob_copy(i, r):
        return pltpu.make_async_copy(prob.at[r], prob_out.at[block(i), r], prob_sem.at[r])

    def act_copy(i):
        return pltpu.make_async_copy(act.at[i % 2], act_out.at[block(i)], act_sem.at[i % 2])

    def slope_copy(i):
        return pltpu.make_async_copy(slope.at[i % 2], slope_out.at[block(i)], slope_sem.at[i % 2])

    def whole_copy(m):
        return pltpu.make_async_copy(whole.at[m], whole_out.at[m], w_sem.at[m])

    x_copy.wait()
    if fused:
        stage(0)

    @pl.loop(0, 4)
    def _(i):
        z = block(i)
        slot = i % 2

        @pl.when(i >= 2)
        def _():
            qkv_copy(i - 2).wait()
            ctx_copy(i - 2).wait()

        @pl.loop(0, 3)
        def _(n):
            add = biases[z, 0:1, tile(n)]
            qkv[slot, :, tile(n)] = (mm(x[...], columns(0, z, n), NN) + add).astype(BF)

        qkv_copy(i).start()

        @pl.loop(0, rows)
        def _(r):
            at = pl.ds(pl.multiple_of(r * length, 32), length)
            pl.when(i >= 1)(lambda: prob_copy(i - 1, r).wait())
            pair = seg_ref[pl.ds(z_own * rows + r, 1), :]
            number = lax.broadcasted_iota(jnp.int32, (8, length), 0)
            among = jnp.where(number == pair, 1.0, 0.0).astype(BF)
            mask = (mm(among, among, TN) - 1.0) * -MASKED
            done = []
            for h in range(heads):
                q = qkv[slot, at, h * HEAD : (h + 1) * HEAD] * jnp.asarray(HEAD ** (-0.5), BF)
                k = qkv[slot, at, width + h * HEAD : width + (h + 1) * HEAD]
                v = qkv[slot, at, 2 * width + h * HEAD : 2 * width + (h + 1) * HEAD]
                scores = mm(k, q, NT) + mask
                weights = jnp.exp(scores - jnp.max(scores, axis=0, keepdims=True))
                share = 1.0 / jnp.sum(weights, axis=0, keepdims=True)
                probs = (weights * share).astype(BF)
                prob[r, h] = probs
                done.append(mm(v, probs, TN).astype(BF).T)
            ctx[slot, at, :] = jnp.concatenate(done, axis=1)
            prob_copy(i, r).start()
            for (a, b), number in ATTEND_STAGES.items():
                pl.when((i == a) & (r == b))(functools.partial(stage, number))

        ctx_copy(i).start()

        @pl.when(i == 0)
        def _():
            @pl.loop(0, strips)
            def _(s):
                value = x[strip(s), :]
                mixed[strip(s), :] = value.astype(F32) + vec[2:3, :]
                turned[0, :, strip(s)] = value.T

            turned_copy(0).start()
            stage(3)

        @pl.loop(0, tokens // CHUNK)
        def _(c):
            at = pl.ds(pl.multiple_of(c * CHUNK, CHUNK), CHUNK)
            add = mm(ctx[slot, at, :], whole[0, z].reshape(D, D)[:, 3 * width :], NT)
            mixed[at, :] = mixed[at, :] + add

    whole_copy(0).start()

    @pl.loop(0, strips)
    def _(s):
        at = strip(s)
        hidden, normal, scale = norm_forward(mixed[at, :], vec[0:1, :], vec[1:2, :])
        normed[at, :] = normal
        rstd[at, :] = jnp.broadcast_to(scale, (STRIP, 128))
        mixed[at, :] = hidden + vec[5:6, :]
        hidden = hidden.astype(BF)
        low[at, :] = hidden
        turned[1, :, at] = hidden.T

    turned_copy(1).start()
    normed_copy = pltpu.make_async_copy(normed, normed_out, end_sem.at[3])
    normed_copy.start()
    rstd_copy = pltpu.make_async_copy(rstd, rstd_out, end_sem.at[4])
    rstd_copy.start()
    if fused:
        gather.local(1).wait()
        gather.local(2).wait()

    @pl.loop(0, 4)
    def _(i):
        z = block(i)
        slot = i % 2

        @pl.when(i >= 2)
        def _():
            act_copy(i - 2).wait()
            slope_copy(i - 2).wait()

        @pl.loop(0, 3)
        def _(n):
            u = mm(low[...], columns(1, z, n), NN) + biases[z, 1:2, tile(n)]
            cumulative = 0.5 + 0.5 * lax.erf(u * SQRT_HALF)
            act[slot, :, tile(n)] = (u * cumulative).astype(BF)
            slope[slot, :, tile(n)] = (cumulative + u * jnp.exp(-0.5 * u * u) * INV_ROOT_TAU).astype(BF)
            for (a, b), number in FEED_STAGES.items():
                pl.when((i == a) & (n == b))(functools.partial(stage, number))

        act_copy(i).start()
        slope_copy(i).start()

        @pl.loop(0, 3)
        def _(n):
            mixed[:, tile(n)] = mixed[:, tile(n)] + mm(act[slot], columns(2, z, n), NN)

        @pl.when(i == 2)
        def _():
            whole_copy(1).start()
            whole_copy(2).start()

    normed_copy.wait()
    cot_copy.wait()
    part[...] = jnp.zeros_like(part)

    @pl.loop(0, strips)
    def _(s):
        at = strip(s)
        block_result, normal, scale = norm_forward(mixed[at, :], vec[3:4, :], vec[4:5, :])
        result[at, :] = block_result.astype(BF)
        back = cot[at, :].astype(F32)
        dsummed = norm_backward(back, vec[3:4, :], normal, scale)
        normed[at, :] = dsummed
        turned[2, :, at] = dsummed.astype(BF).T
        part[3:4, :] += jnp.sum(back * normal, axis=0, keepdims=True)
        part[4:5, :] += jnp.sum(back, axis=0, keepdims=True)
        part[5:6, :] += jnp.sum(dsummed, axis=0, keepdims=True)

    last = [
        turned_copy(2),
        pltpu.make_async_copy(normed, ds_out, end_sem.at[5]),
        pltpu.make_async_copy(result, result_out, end_sem.at[6]),
        pltpu.make_async_copy(part, part_out, end_sem.at[7]),
    ]
    for copy in last:
        copy.start()
    for i in (2, 3):
        qkv_copy(i).wait()
        ctx_copy(i).wait()
        act_copy(i).wait()
        slope_copy(i).wait()
    for r in range(rows):
        prob_copy(3, r).wait()
    turned_copy(0).wait()
    turned_copy(1).wait()
    rstd_copy.wait()
    for m in range(3):
        whole_copy(m).wait()
    for copy in last:
        copy.wait()
    if fused:
        gather.finish()


def run_forward(x, cot, segments, vector_params, weights, biases):
    rows, length, _ = x.shape
    tokens = rows * length
    fused = lax.axis_size("dp") == 8 and lax.axis_size("mp") == 4
    hbm, vmem = pl.BlockSpec(memory_space=pl.ANY), pl.BlockSpec(memory_space=pltpu.VMEM)
    flat = (tokens, D)
    width = D // 4
    block = (4, 2, SLICE, D)
    dense = [x.reshape(flat), cot.reshape(flat), segments, vector_params]
    if fused:
        triple, output, expand, shrink = weights
        held = [triple.transpose(0, 2, 1), output, expand.reshape(block), shrink.reshape(block)]
        held = held + [biases[0].transpose(1, 0, 2), biases[1]]
        spaces = [hbm, hbm, hbm, hbm, vmem, vmem]
    else:
        mats = pack_weights(*weights)
        held = [jnp.stack([lax.all_gather(m, "mp", axis=0) for m in mats]).reshape((3, 4) + block)]
        held = held + [lax.all_gather(pack_biases(*biases), "mp", axis=0)]
        spaces = [hbm, hbm]
    probs = (rows, D // HEAD // 4, length, length)
    shape = jax.ShapeDtypeStruct
    dma = pltpu.SemaphoreType.DMA
    return pl.pallas_call(
        functools.partial(forward_kernel, fused, rows, length),
        out_shape=(
            shape((3, 4) + block, BF),
            shape((4,) + flat, BF),
            shape((4, tokens, width), BF),
            shape((4,) + probs, BF),
            shape((4,) + flat, BF),
            shape((4,) + flat, BF),
            shape(flat, F32),
            shape((tokens, 128), F32),
            shape(flat, F32),
            shape((3, D, tokens), BF),
            shape(flat, BF),
            shape((VECTORS, D), F32),
        ),
        in_specs=[hbm, hbm, vmem, vmem] + spaces,
        out_specs=(hbm,) * 12,
        scratch_shapes=([dma(s) for s in Gather.sems] if fused else [])
        + [
            pltpu.VMEM((3, 4) + block, BF),
            pltpu.VMEM((VECTORS, D), F32),
            pltpu.VMEM((4, VECTORS, D), F32),
            pltpu.VMEM((D, D), BF),
            pltpu.VMEM((VECTORS, D), F32),
            pltpu.VMEM(flat, BF),
            pltpu.VMEM(flat, BF),
            pltpu.VMEM((2,) + flat, BF),
            pltpu.VMEM((2, tokens, width), BF),
            pltpu.VMEM(probs, BF),
            pltpu.VMEM((2,) + flat, BF),
            pltpu.VMEM((2,) + flat, BF),
            pltpu.VMEM(flat, F32),
            pltpu.VMEM(flat, F32),
            pltpu.VMEM((tokens, 128), F32),
            pltpu.VMEM(flat, BF),
            pltpu.VMEM((3, D, tokens), BF),
            pltpu.VMEM(flat, BF),
            pltpu.VMEM((VECTORS, D), F32),
            dma((6,)),
            dma((3,)),
            dma((2,)),
            dma((2,)),
            dma((rows,)),
            dma((2,)),
            dma((2,)),
            dma((8,)),
        ],
        compiler_params=pltpu.CompilerParams(
            collective_id=0 if fused else None, has_side_effects=True, vmem_limit_bytes=VMEM_MOST
        ),
        name="forward",
    )(*dense, *held)


def backward_kernel(fused, rows, length, *refs):
    n_sem = len(Scatter.sems) if fused else 0
    n_buf = len(Scatter.buffers) if fused else 0
    (vec_in, part_in, whole, qkv_in, ctx_in, prob_in, act_in, slope_in, normed_in, rstd_in, ds_in, turned_in) = refs[:12]
    grad_out, small_out, input_out = refs[12:15]
    rest = refs[15:]
    buffers, sems, rest = rest[:n_buf], rest[n_buf : n_buf + n_sem], rest[n_buf + n_sem :]
    (grads, weights, wide, tall, dexp, stream, normed, rstd, low, turned, prob, ctx, dctx, part, vec,
     w_sem, wide_sem, tall_sem, prob_sem, ctx_sem, turned_sem, end_sem) = rest
    tokens = rows * length
    strips = tokens // STRIP
    heads = D // HEAD // 4
    width = heads * HEAD

    def weight_copy(m, z, slot):
        return pltpu.make_async_copy(whole.at[m, z], weights.at[slot], w_sem.at[slot])

    def wide_copy(source, z):
        return pltpu.make_async_copy(source.at[z], wide.at[z % 2], wide_sem.at[z % 2])

    def tall_copy(z):
        return pltpu.make_async_copy(slope_in.at[z], tall.at[z % 2], tall_sem.at[z % 2])

    def turned_copy(source, slot):
        return pltpu.make_async_copy(turned_in.at[source], turned.at[slot], turned_sem.at[slot])

    def prob_copy(g):
        return pltpu.make_async_copy(prob_in.at[g // rows, g % rows], prob.at[g % 2], prob_sem.at[g % 2])

    def ctx_copy(z):
        return pltpu.make_async_copy(ctx_in.at[z], ctx.at[z % 2], ctx_sem.at[z % 2])

    stream_copy = pltpu.make_async_copy(ds_in, stream, end_sem.at[0])
    normed_copy = pltpu.make_async_copy(normed_in, normed, end_sem.at[1])
    rstd_copy = pltpu.make_async_copy(rstd_in, rstd, end_sem.at[2])
    turned_copy(2, 0).start()
    wide_copy(act_in, 0).start()
    stream_copy.start()
    weight_copy(2, 0, 0).start()
    tall_copy(0).start()
    turned_copy(1, 1).start()
    weight_copy(1, 0, 1).start()
    wide_copy(act_in, 1).start()
    tall_copy(1).start()
    weight_copy(2, 1, 2).start()
    weight_copy(1, 1, 3).start()
    normed_copy.start()
    rstd_copy.start()
    if fused:
        scatter = Scatter(grads, buffers, sems)
        scatter.begin()
        stage = scatter.stage
    else:
        stage = lambda i: None
    vec[0:6, :] = vec_in[...].astype(F32)
    part[...] = jnp.zeros_like(part)
    part[0:VECTORS, :] = part_in[...]

    def outer(slot, turned_slot, right, lanes, offset=0, size=TILE):
        product = mm(turned[turned_slot], right[:, lanes], NN).astype(BF)
        grads[slot, :, :, :, offset if size != TILE else lanes] = product.reshape(4, 2, SLICE, size)

    def emit(slot, m, z):
        if not fused:
            copy = pltpu.make_async_copy(grads.at[slot], grad_out.at[m, z], end_sem.at[3])
            copy.start()
            copy.wait()

    turned_copy(2, 0).wait()

    @pl.loop(0, 4)
    def _(z):
        half = z % 2
        slot = 2 * half
        wide_copy(act_in, z).wait()
        pl.loop(0, 3)(lambda n: outer(z, 0, wide.at[half], tile(n)))
        emit(z, 2, z)
        for k in range(4):
            pl.when(z == k)(functools.partial(stage, 2 * k))

        @pl.when(z == 0)
        def _():
            stream_copy.wait()

            @pl.loop(0, strips)
            def _(s):
                low[strip(s), :] = stream[strip(s), :].astype(BF)

            turned_copy(1, 1).wait()

        weight_copy(2, z, slot).wait()
        tall_copy(z).wait()

        @pl.loop(0, 3)
        def _(n):
            dactive = mm(low[...], weights[slot, tile(n), :], NT)
            value = (dactive * tall[half, :, tile(n)].astype(F32)).astype(BF)
            dexp[:, tile(n)] = value
            part[pl.ds(10 + z, 1), tile(n)] = jnp.sum(value.astype(F32), axis=0, keepdims=True)

        pl.loop(0, 3)(lambda n: outer(4 + z, 1, dexp, tile(n)))
        emit(4 + z, 1, z)
        for k in range(4):
            pl.when(z == k)(functools.partial(stage, 2 * k + 1))
        weight_copy(1, z, slot + 1).wait()

        @pl.loop(0, 3)
        def _(n):
            stream[:, tile(n)] = stream[:, tile(n)] + mm(dexp[...], weights[slot + 1, tile(n), :], NT)

        @pl.when(z < 2)
        def _():
            wide_copy(act_in, z + 2).start()
            tall_copy(z + 2).start()
            weight_copy(2, z + 2, slot).start()
            weight_copy(1, z + 2, slot + 1).start()

        @pl.when(z == 2)
        def _():
            wide_copy(qkv_in, 0).start()
            weight_copy(0, 0, 0).start()
            weight_copy(0, 1, 1).start()
            ctx_copy(0).start()
            ctx_copy(1).start()
            prob_copy(0).start()

        @pl.when(z == 3)
        def _():
            wide_copy(qkv_in, 1).start()
            weight_copy(0, 2, 2).start()
            weight_copy(0, 3, 3).start()
            turned_copy(0, 0).start()

    normed_copy.wait()
    rstd_copy.wait()

    @pl.loop(0, strips)
    def _(s):
        at = strip(s)
        dhidden, normal = stream[at, :], normed[at, :]
        dmixed = norm_backward(dhidden, vec[0:1, :], normal, rstd[at, 0:1])
        part[0:1, :] += jnp.sum(dhidden * normal, axis=0, keepdims=True)
        part[1:2, :] += jnp.sum(dhidden, axis=0, keepdims=True)
        part[2:3, :] += jnp.sum(dmixed, axis=0, keepdims=True)
        stream[at, :] = dmixed
        dmixed = dmixed.astype(BF)
        low[at, :] = dmixed
        turned[1, :, at] = dmixed.T

    turned_copy(0, 0).wait()
    dproj = tall
    dproj[:, :, 2 * TILE : D] = jnp.zeros((2, tokens, TILE), BF)

    def pull(z):
        @pl.loop(0, 3)
        def _(n):
            add = mm(dproj[z % 2, :, 0 : 3 * width], weights[z, tile(n), 0 : 3 * width], NT)
            stream[:, tile(n)] = stream[:, tile(n)] + add

    @pl.loop(0, 4)
    def _(z):
        half = z % 2
        weight_copy(0, z, z).wait()
        wide_copy(qkv_in, z).wait()
        ctx_copy(z).wait()
        dctx[...] = mm(low[...], weights[z, :, 3 * width :], NN).astype(BF)

        @pl.loop(0, rows)
        def _(r):
            at = pl.ds(pl.multiple_of(r * length, 32), length)
            g = z * rows + r
            prob_copy(g).wait()
            pl.when(g + 1 < 4 * rows)(lambda: prob_copy(g + 1).start())
            dq, dk, dv = [], [], []
            scale = jnp.asarray(HEAD ** (-0.5), BF)
            for h in range(heads):
                q = wide[half, at, h * HEAD : (h + 1) * HEAD] * scale
                k = wide[half, at, width + h * HEAD : width + (h + 1) * HEAD]
                v = wide[half, at, 2 * width + h * HEAD : 2 * width + (h + 1) * HEAD]
                dc = dctx[at, h * HEAD : (h + 1) * HEAD]
                probs = prob[g % 2, h]
                full = probs.astype(F32)
                dprobs = mm(v, dc, NT)
                inner = jnp.sum(full * dprobs, axis=0, keepdims=True)
                dscores = (full * (dprobs - inner)).astype(BF)
                dv.append(mm(probs, dc, NN).astype(BF))
                dk.append(mm(dscores, q, NN).astype(BF))
                dq.append((mm(k, dscores, TN) * HEAD ** (-0.5)).astype(BF).T)
            joined = jnp.concatenate(dq + dk + dv, axis=1)
            dproj[half, at, 0 : 3 * width] = joined
            line = pl.ds(6 + z, 1)
            before = jnp.where(r == 0, 0.0, part[line, 0 : 3 * width])
            part[line, 0 : 3 * width] = before + jnp.sum(joined.astype(F32), axis=0, keepdims=True)

        if fused:
            for k in range(4):
                pl.when(z == k)(lambda k=k: scatter.to_core(2 * k).wait_send())
        pl.loop(0, 3)(lambda n: outer(z, 0, dproj.at[half], tile(n)))
        outer(z, 1, ctx.at[half], slice(None), slice(3 * width, D), width)
        emit(z, 0, z)
        for k in range(4):
            pl.when(z == k)(functools.partial(stage, 8 + k))

        @pl.when(z < 2)
        def _():
            wide_copy(qkv_in, z + 2).start()
            ctx_copy(z + 2).start()
            pull(z)

    if fused:
        n = len(Scatter.steps)
        scatter.small_stage(part, 0)
    pull(2)
    if fused:
        stage(n)
        scatter.small_stage(part, 1)
    pull(3)
    input_copy = pltpu.make_async_copy(stream, input_out, end_sem.at[0])
    input_copy.start()
    if fused:
        stage(n + 1)
        scatter.small_stage(part, 2)
        grad_out[2] = scatter.total(2)
        scatter.small_stage(part, 3)
        stage(n + 2)
        grad_out[1] = scatter.total(1)
        small_out[...] = scatter.small_stage(part, 4)
        grad_out[0] = scatter.total(0)
        scatter.finish(part)
    else:
        small_out[...] = part[...]
    input_copy.wait()


def run_backward(vector_params, part, saved, rows, length):
    fused = lax.axis_size("dp") == 8 and lax.axis_size("mp") == 4
    hbm, vmem = pl.BlockSpec(memory_space=pl.ANY), pl.BlockSpec(memory_space=pltpu.VMEM)
    tokens = rows * length
    flat = (tokens, D)
    width = D // 4
    block = (4, 2, SLICE, D)
    shape = jax.ShapeDtypeStruct
    dma = pltpu.SemaphoreType.DMA
    whole_grad = shape((3, SLICE, D), F32) if fused else shape((3, 4) + block, BF)
    saved = [saved[0].reshape(3, 4, D, D)] + list(saved[1:])
    grads, sums, input_grad = pl.pallas_call(
        functools.partial(backward_kernel, fused, rows, length),
        out_shape=(whole_grad, shape((SMALL, D), F32), shape(flat, F32)),
        in_specs=[vmem] * 2 + [hbm] * 10,
        out_specs=(vmem if fused else hbm, vmem, hbm),
        scratch_shapes=([pltpu.VMEM(s, t) for s, t in Scatter.buffers] + [dma(s) for s in Scatter.sems] if fused else [])
        + [
            pltpu.VMEM((8,) + block, BF),
            pltpu.VMEM((4, D, D), BF),
            pltpu.VMEM((2,) + flat, BF),
            pltpu.VMEM((2,) + flat, BF),
            pltpu.VMEM(flat, BF),
            pltpu.VMEM(flat, F32),
            pltpu.VMEM(flat, F32),
            pltpu.VMEM((tokens, 128), F32),
            pltpu.VMEM(flat, BF),
            pltpu.VMEM((2, D, tokens), BF),
            pltpu.VMEM((2, D // HEAD // 4, length, length), BF),
            pltpu.VMEM((2, tokens, width), BF),
            pltpu.VMEM((tokens, width), BF),
            pltpu.VMEM((SMALL, D), F32),
            pltpu.VMEM((VECTORS, D), F32),
            dma((4,)),
            dma((2,)),
            dma((2,)),
            dma((2,)),
            dma((2,)),
            dma((2,)),
            dma((4,)),
        ],
        compiler_params=pltpu.CompilerParams(
            collective_id=1 if fused else None, has_side_effects=True, vmem_limit_bytes=VMEM_MOST
        ),
        name="backward",
    )(vector_params, part, *saved)
    if not fused:
        parts = lax.axis_size("dp")
        grads = lax.psum_scatter(grads.reshape(3, 4, D, D), "dp", scatter_dimension=2, tiled=True)
        grads = lax.psum_scatter(grads, "mp", scatter_dimension=1, tiled=True)
        grads = grads.reshape(3, D // parts, D).astype(F32)
        sums = lax.psum(sums, ("dp", "mp"))
    return input_grad, grads, sums


RATES = (D ** (-0.5), 0.5, (D // 16) ** (-0.5), D ** (-0.5), 0.5, FF ** (-0.5), 0.3)


def update_kernel(reduced, sums, result_in, input_in, *refs):
    state, outs, result_out, input_out, result, input_grad, sems = refs[:21], refs[21:49], *refs[49:]
    moves = [
        (pltpu.make_async_copy(input_in, input_grad, sems.at[0]), pltpu.make_async_copy(input_grad, input_out, sems.at[1])),
        (pltpu.make_async_copy(result_in, result, sems.at[2]), pltpu.make_async_copy(result, result_out, sems.at[3])),
    ]
    for load, _ in moves:
        load.start()
    dp, mp = lax.axis_index("dp"), lax.axis_index("mp")
    groups = lax.axis_size("mp")
    width = D // groups
    own = width // HEAD

    def update(i, gradient, at=Ellipsis):
        new = adam_update(*(state[3 * i + j][at] for j in range(3)), gradient, RATES[i])
        for j in range(4):
            outs[4 * i + j][at] = new[j]

    update(3, reduced[1])
    for load, store in moves:
        load.wait()
        store.start()
    mixing = reduced[0]
    for j in range(3):
        update(0, mixing[:, j * width : (j + 1) * width], j)
    update(2, mixing[:, 3 * width :].T)
    update(5, reduced[2])

    def lanes(row, count, start):
        return pltpu.roll(sums[pl.ds(row, count), :], lax.rem(D - start, D), 1)

    piece = state[3].shape[2]
    moved = lanes(6 + mp, 1, dp * piece)
    for j in (0, 1):
        for h in range(own):
            at = 2 * j * width + h * HEAD
            update(1, moved[:, at : at + piece], (h, slice(j, j + 1)))
    piece = state[12].shape[0]
    moved = lanes(10 + mp, 1, dp * piece)
    blocks = [moved[:, b * HEAD : b * HEAD + piece] for b in range(D // HEAD)]
    update(4, jnp.concatenate(blocks, axis=0).T)
    piece = state[18].shape[1]
    update(6, lanes(0, 8, (dp * groups + mp) * piece)[0:6, 0:piece])
    for _, store in moves:
        store.wait()


AXES = ((0, 1, 2), (1, 0, 2), (0, 1), (0, 1), (1, 0), (1, 0), (0, 1))


def update_all(state, reduced, sums, result, input_grad):
    hbm, vmem = pl.BlockSpec(memory_space=pl.ANY), pl.BlockSpec(memory_space=pltpu.VMEM)
    state = [s.transpose(AXES[i // 3]) for i, s in enumerate(state)]
    shapes = []
    for i in range(7):
        shapes = shapes + [jax.ShapeDtypeStruct(state[3 * i].shape, t) for t in (F32, F32, F32, BF)]
    kept = [jax.ShapeDtypeStruct(a.shape, a.dtype) for a in (result, input_grad)]
    *new, result, input_grad = pl.pallas_call(
        update_kernel,
        out_shape=tuple(shapes + kept),
        in_specs=[vmem] * 2 + [hbm] * 2 + [vmem] * 21,
        out_specs=(vmem,) * 28 + (hbm,) * 2,
        scratch_shapes=[pltpu.VMEM(a.shape, a.dtype) for a in kept] + [pltpu.SemaphoreType.DMA((4,))],
        name="update",
    )(reduced, sums, result, input_grad, *state)
    return result, input_grad, tuple(s.transpose(AXES[i // 4]) for i, s in enumerate(new))


def per_device(
    activations,
    cotangent,
    segments,
    triple_weight,
    query_value_bias,
    output_weight,
    expand_weight,
    expand_bias,
    shrink_weight,
    vector_params,
    *state,
):
    rows, length, _ = activations.shape
    weights = (triple_weight, output_weight, expand_weight, shrink_weight)
    *saved, result, part = run_forward(
        activations, cotangent, segments, vector_params, weights, (query_value_bias, expand_bias)
    )
    input_grad, reduced, sums = run_backward(vector_params, part, saved, rows, length)
    result, input_grad, new = update_all(state, reduced, sums, result, input_grad)
    return (result.reshape(activations.shape), input_grad.reshape(activations.shape)) + new


STATE_SPECS = (
    P(None, "dp", "mp"),
    P(None, "mp", "dp"),
    P("mp", "dp"),
    P("dp", "mp"),
    P("mp", "dp"),
    P("mp", "dp"),
    P(None, ("dp", "mp")),
)


def solution(mesh):
    rows = P(("dp", "mp"), None, None)
    placed = (
        rows,
        rows,
        P("dp", None),
        P(None, None, "mp"),
        P(None, "mp", None),
        P("mp", None),
        P(None, "mp"),
        P("mp", None),
        P("mp", None),
        P(),
    )
    for spec in STATE_SPECS:
        placed = placed + (spec,) * 3
    out_specs = (rows, rows)
    for spec in STATE_SPECS:
        out_specs = out_specs + (spec,) * 4
    return jax.shard_map(per_device, mesh=mesh, in_specs=placed, out_specs=out_specs, check_vma=False)
```

profile of v0, /device:TPU:0, one launch (start us, length us, event | category | flops | bytes accessed | tf_op | source)
XLA Modules:
  0.0 224.0 jit_solution(7650006392716280631)
XLA Ops:
  0.7 102.5 %forward.1 = (bf16[3,4,4,2,96,768]{5,4,3,2,1,0:T(8,128)(2,1)}, bf16[4,1152,768]{2,1,0:T(8,128)(2,1)}, bf16[4,1152,192]{2,1,0:T(8,128)(2,1)}, bf16[4,4,3,288,288]...) custom-call(bf16[1152,768]{1,0:T(8,128)(2,1)} %bitcast.31, ...), custom_call_target="tpu_custom_call" | custom-call | tf_op jit(solution)/shard_map/forward/pallas_call | solution.py:601
  103.2 112.1 %backward.1 = (f32[3,96,768]{2,1,0:T(8,128)}, f32[16,768]{1,0:T(8,128)}, f32[1152,768]{1,0:T(8,128)}) custom-call(bf16[6,768]{1,0:T(8,128)(2,1)} %refs_0_.2, f32[8,768]{1,0:T(8,128)} %get-tuple-element.75.refs_1_, bf16[3,4,768,768]{3,2,1,0:T(8,128)(2,1)} %bitcast.30, bf16[4,1152,768]{2,1,0:T(8,128)(2,1)} %get-tuple-element.77.refs_3_, ...), custom_call_target="tpu_custom_call" | custom-call | tf_op jit(solution)/shard_map/backward/pallas_call | solution.py:901
  215.3 8.5 %update.1 = (f32[3,96,192]{2,1,0:T(8,128)}, f32[3,96,192]{2,1,0:T(8,128)}, f32[3,96,192]{2,1,0:T(8,128)}, bf16[3,96,192]{2,1,0:T(8,128)(2,1)}, f32[3,2,8]{2,1,0:...) custom-call(f32[3,96,768]{2,1,0:T(8,128)} %get-tuple-element.86.redu, ...), custom_call_target="tpu_custom_call" | custom-call | tf_op jit(solution)/shard_map/update/pallas_call | solution.py:1005
where the time goes:
time: 228 us; the launch traced here: 224 us
  Pallas kernels  223 us (98%)
    pallas_call x1, Pallas kernels, run_backward(): pl.pallas_call(functools.partial(backward_kernel, fused, rows, length), o...  112 us
    pallas_call x1, Pallas kernels, run_forward(): pl.pallas_call(functools.partial(forward_kernel, fused, rows, length), ou...  103 us
    pallas_call x1, Pallas kernels, update_all(): pl.pallas_call(update_kernel, out_shape=tuple(shapes + kept), in_specs=[v...  8.5 us

commit v1 on v0

--- a/solution.py
+++ b/solution.py
@@ -127,10 +127,9 @@
             self.along_z(0, d).start()
             self.small(d).start()
 
-    def stage(self, i):
-        steps, n = self.steps, len(self.steps)
-        if i < n:
-            m, d = steps[i]
+    def run(self, kind, i):
+        m, d = self.steps[i]
+        if kind == 0:
             self.along_z(m, d).wait_recv()
             if i < 3:
                 self.small(d).wait_recv()
@@ -138,17 +137,17 @@
             self.to_y(m, d).start()
             if m < 2:
                 self.along_z(m + 1, d).start()
-        if 0 <= i - 1 < n:
-            self.to_x(*steps[i - 1]).wait_recv()
-            self.to_y(*steps[i - 1]).wait_recv()
-            self.on_to_y(*steps[i - 1]).start()
-            self.on_to_x(*steps[i - 1]).start()
-        if 0 <= i - 2 < n:
-            self.on_to_y(*steps[i - 2]).wait_recv()
-            self.on_to_x(*steps[i - 2]).wait_recv()
-            self.to_core(*steps[i - 2]).start()
-        if 0 <= i - 3 < n:
-            self.to_core(*steps[i - 3]).wait_recv()
+        elif kind == 1:
+            self.to_x(m, d).wait_recv()
+            self.to_y(m, d).wait_recv()
+            self.on_to_y(m, d).start()
+            self.on_to_x(m, d).start()
+        elif kind == 2:
+            self.on_to_y(m, d).wait_recv()
+            self.on_to_x(m, d).wait_recv()
+            self.to_core(m, d).start()
+        else:
+            self.to_core(m, d).wait_recv()
 
     def finish(self):
         for d in (1, 2, 3):
@@ -159,7 +158,7 @@
 
 
 class Scatter:
-    steps = [(m, k) for k in range(4) for m in (2, 1)] + [(0, k) for k in range(4)]
+    steps = [(m, k) for k in (0, 3, 2, 1) for m in (2, 1)] + [(0, k) for k in (0, 3, 2, 1)]
     slots = [k + 4 * j for k in range(4) for j in (0, 1)] + list(range(4))
     buffers = [((12, 4, SLICE, D), BF)] + [((12, 2, HALF, D), BF)] * 2 + [((12, HALF, D), BF)] * 2 + [
         ((3, 3, SLICE, D), BF), ((3, 4, SLICE, D), BF), ((6, SMALL, D), F32), ((3, SMALL, D), F32)]
@@ -205,14 +204,12 @@
         p, z, _, _, pc, px, py = self.where[:7]
         greet(p, z, pc, px, py)
 
-    def stage(self, i):
-        n = len(self.steps)
+    def run(self, kind, j):
         core, xy, xyx, xyy = self.where[2], self.where[3], self.where[7], self.where[8]
         low, high = slice(0, HALF), slice(HALF, SLICE)
-        if i < n:
-            self.to_core(i).start()
-        j = i - 1
-        if 0 <= j < n:
+        if kind == 0:
+            self.to_core(j).start()
+        elif kind == 1:
             self.to_core(j).wait_recv()
 
             @pl.loop(0, 4)
@@ -220,11 +217,10 @@
                 mine = self.grads[self.slots[j], q, core].astype(F32)
                 self.sum[j, q] = (self.sum[j, q].astype(F32) + mine).astype(BF)
 
-            for t in (0, 1):
+            for t in (1, 0):
                 self.to_x(j, t).start()
                 self.to_y(j, t).start()
-        j = i - 2
-        if 0 <= j < n:
+        elif kind == 2:
             for t in (0, 1):
                 self.to_x(j, t).wait_recv()
                 self.to_y(j, t).wait_recv()
@@ -232,8 +228,7 @@
             self.sum[j, xyx, high] = (self.sum[j, xyx, high].astype(F32) + self.ry[j, 1].astype(F32)).astype(BF)
             self.on_to_y(j).start()
             self.on_to_x(j).start()
-        j = i - 3
-        if 0 <= j < n:
+        else:
             m, k = self.steps[j]
             self.on_to_y(j).wait_recv()
             self.on_to_x(j).wait_recv()
@@ -319,8 +314,16 @@
 STRIP = 128
 TILE = 256
 VMEM_MOST = 60 << 20
-ATTEND_STAGES = {(0, 1): 1, (0, 3): 2, (1, 1): 4, (2, 0): 5, (2, 3): 6, (3, 2): 7}
-FEED_STAGES = {(0, 0): 8, (0, 2): 9, (1, 0): 10, (1, 2): 11}
+EVENTS = {
+    "block": {(1, 0): ((1, 0), (0, 1), (2, 0), (0, 2), (3, 0)), (2, 0): ((0, 5), (1, 3), (3, 1)), (3, 0): ((2, 3),)},
+    "project": {(1, 2): ((1, 1),)},
+    "attend": {(0, 3): ((0, 0),), (1, 0): ((0, 3),), (1, 2): ((1, 2),), (1, 3): ((2, 1),), (2, 0): ((2, 2), (0, 7)), (2, 3): ((1, 5), (0, 4), (3, 2)), (3, 1): ((1, 7), (3, 3)), (3, 2): ((2, 5), (0, 6))},
+    "turn": {},
+    "norm": {(0, 0): ((1, 4), (0, 8), (3, 5), (2, 7))},
+    "feed": {(1, 0): ((1, 8), (3, 4)), (2, 0): ((3, 6),)},
+    "expand": {(0, 2): ((1, 6),), (1, 2): ((2, 6),), (2, 2): ((3, 8),)},
+    "shrink": {(0, 1): ((3, 7),), (0, 2): ((2, 4),), (1, 1): ((2, 8),)},
+}
 
 
 def tile(n):
@@ -359,7 +362,6 @@
         for copy in joint_copies:
             copy.start()
         gather = Gather((e_ref, s_ref), whole, bias, biases, gather_sems)
-        stage = gather.stage
         bias[...] = jnp.zeros_like(bias)
         for h in range(heads):
             for j in (0, 1):
@@ -385,7 +387,6 @@
         small.start()
         copy.wait()
         small.wait()
-        stage = lambda i: None
     cot_copy.start()
     vec[0:6, :] = vec_in[...].astype(F32)
 
@@ -416,12 +417,19 @@
     def whole_copy(m):
         return pltpu.make_async_copy(whole.at[m], whole_out.at[m], w_sem.at[m])
 
+    def events(place, i=0, n=0):
+        for (a, b), due in EVENTS[place].items() if fused else ():
+
+            @pl.when((i == a) & (n == b))
+            def _(due=due):
+                for kind, step in due:
+                    gather.run(kind, step)
+
     x_copy.wait()
-    if fused:
-        stage(0)
 
     @pl.loop(0, 4)
     def _(i):
+        events("block", i)
         z = block(i)
         slot = i % 2
 
@@ -434,6 +442,7 @@
         def _(n):
             add = biases[z, 0:1, tile(n)]
             qkv[slot, :, tile(n)] = (mm(x[...], columns(0, z, n), NN) + add).astype(BF)
+            events("project", i, n)
 
         qkv_copy(i).start()
 
@@ -458,8 +467,7 @@
                 done.append(mm(v, probs, TN).astype(BF).T)
             ctx[slot, at, :] = jnp.concatenate(done, axis=1)
             prob_copy(i, r).start()
-            for (a, b), number in ATTEND_STAGES.items():
-                pl.when((i == a) & (r == b))(functools.partial(stage, number))
+            events("attend", i, r)
 
         ctx_copy(i).start()
 
@@ -472,7 +480,7 @@
                 turned[0, :, strip(s)] = value.T
 
             turned_copy(0).start()
-            stage(3)
+            events("turn")
 
         @pl.loop(0, tokens // CHUNK)
         def _(c):
@@ -493,6 +501,7 @@
         low[at, :] = hidden
         turned[1, :, at] = hidden.T
 
+    events("norm")
     turned_copy(1).start()
     normed_copy = pltpu.make_async_copy(normed, normed_out, end_sem.at[3])
     normed_copy.start()
@@ -504,6 +513,7 @@
 
     @pl.loop(0, 4)
     def _(i):
+        events("feed", i)
         z = block(i)
         slot = i % 2
 
@@ -518,8 +528,7 @@
             cumulative = 0.5 + 0.5 * lax.erf(u * SQRT_HALF)
             act[slot, :, tile(n)] = (u * cumulative).astype(BF)
             slope[slot, :, tile(n)] = (cumulative + u * jnp.exp(-0.5 * u * u) * INV_ROOT_TAU).astype(BF)
-            for (a, b), number in FEED_STAGES.items():
-                pl.when((i == a) & (n == b))(functools.partial(stage, number))
+            events("expand", i, n)
 
         act_copy(i).start()
         slope_copy(i).start()
@@ -527,6 +536,7 @@
         @pl.loop(0, 3)
         def _(n):
             mixed[:, tile(n)] = mixed[:, tile(n)] + mm(act[slot], columns(2, z, n), NN)
+            events("shrink", i, n)
 
         @pl.when(i == 2)
         def _():
@@ -653,6 +663,23 @@
     )(*dense, *held)
 
 
+BACK_EVENTS = {
+    "shrink": {(0, 2): ((0, 0),), (1, 2): ((0, 2),), (2, 2): ((0, 4),), (3, 1): ((3, 1),), (3, 2): ((0, 6),)},
+    "slope": {(1, 1): ((1, 1),), (2, 0): ((2, 1), (1, 3)), (2, 2): ((3, 0),), (3, 0): ((1, 5),), (3, 2): ((2, 3),)},
+    "expand": {(0, 2): ((0, 1), (1, 0)), (1, 1): ((2, 0),), (1, 2): ((0, 3), (1, 2)), (2, 2): ((0, 5), (1, 4)), (3, 2): ((0, 7), (1, 6))},
+    "hidden": {(2, 1): ((2, 2),), (3, 2): ((2, 4),)},
+    "norm": {(0, 0): ((3, 2), (1, 7))},
+    "attend": {(0, 0): ((2, 5),), (0, 1): ((3, 3),), (1, 1): ((2, 7), (1, 8)), (1, 2): ((3, 5),), (2, 1): ((2, 8), (1, 9)), (3, 2): ((2, 9),), (3, 3): ((1, 10),)},
+    "project": {(0, 0): ((0, 8), (2, 6)), (1, 0): ((0, 9), (3, 6), (3, 7)), (2, 0): ((0, 10), (3, 8)), (3, 0): ((0, 11),)},
+    "pull": {(0, 1): ((3, 4),), (2, 2): ((3, 9),)},
+    "last": {(0, 0): ((1, 11), (2, 10), (2, 11), (3, 10), (3, 11))},
+}
+
+
+def turn_block(j):
+    return 3 * j % 4
+
+
 def backward_kernel(fused, rows, length, *refs):
     n_sem = len(Scatter.sems) if fused else 0
     n_buf = len(Scatter.buffers) if fused else 0
@@ -667,23 +694,23 @@
     heads = D // HEAD // 4
     width = heads * HEAD
 
-    def weight_copy(m, z, slot):
-        return pltpu.make_async_copy(whole.at[m, z], weights.at[slot], w_sem.at[slot])
-
-    def wide_copy(source, z):
-        return pltpu.make_async_copy(source.at[z], wide.at[z % 2], wide_sem.at[z % 2])
-
-    def tall_copy(z):
-        return pltpu.make_async_copy(slope_in.at[z], tall.at[z % 2], tall_sem.at[z % 2])
+    def weight_copy(m, j, slot):
+        return pltpu.make_async_copy(whole.at[m, turn_block(j)], weights.at[slot], w_sem.at[slot])
+
+    def wide_copy(source, j):
+        return pltpu.make_async_copy(source.at[turn_block(j)], wide.at[j % 2], wide_sem.at[j % 2])
+
+    def tall_copy(j):
+        return pltpu.make_async_copy(slope_in.at[turn_block(j)], tall.at[j % 2], tall_sem.at[j % 2])
 
     def turned_copy(source, slot):
         return pltpu.make_async_copy(turned_in.at[source], turned.at[slot], turned_sem.at[slot])
 
     def prob_copy(g):
-        return pltpu.make_async_copy(prob_in.at[g // rows, g % rows], prob.at[g % 2], prob_sem.at[g % 2])
-
-    def ctx_copy(z):
-        return pltpu.make_async_copy(ctx_in.at[z], ctx.at[z % 2], ctx_sem.at[z % 2])
+        return pltpu.make_async_copy(prob_in.at[turn_block(g // rows), g % rows], prob.at[g % 2], prob_sem.at[g % 2])
+
+    def ctx_copy(j):
+        return pltpu.make_async_copy(ctx_in.at[turn_block(j)], ctx.at[j % 2], ctx_sem.at[j % 2])
 
     stream_copy = pltpu.make_async_copy(ds_in, stream, end_sem.at[0])
     normed_copy = pltpu.make_async_copy(normed_in, normed, end_sem.at[1])
@@ -704,9 +731,15 @@
     if fused:
         scatter = Scatter(grads, buffers, sems)
         scatter.begin()
-        stage = scatter.stage
-    else:
-        stage = lambda i: None
+
+    def events(place, j=0, n=0):
+        for (a, c), due in BACK_EVENTS[place].items() if fused else ():
+
+            @pl.when((j == a) & (n == c))
+            def _(due=due):
+                for kind, step in due:
+                    scatter.run(kind, step)
+
     vec[0:6, :] = vec_in[...].astype(F32)
     part[...] = jnp.zeros_like(part)
     part[0:VECTORS, :] = part_in[...]
@@ -724,16 +757,20 @@
     turned_copy(2, 0).wait()
 
     @pl.loop(0, 4)
-    def _(z):
-        half = z % 2
+    def _(j):
+        half = j % 2
         slot = 2 * half
-        wide_copy(act_in, z).wait()
-        pl.loop(0, 3)(lambda n: outer(z, 0, wide.at[half], tile(n)))
-        emit(z, 2, z)
-        for k in range(4):
-            pl.when(z == k)(functools.partial(stage, 2 * k))
-
-        @pl.when(z == 0)
+        z = turn_block(j)
+        wide_copy(act_in, j).wait()
+
+        @pl.loop(0, 3)
+        def _(n):
+            outer(j, 0, wide.at[half], tile(n))
+            events("shrink", j, n)
+
+        emit(j, 2, z)
+
+        @pl.when(j == 0)
         def _():
             stream_copy.wait()
 
@@ -743,8 +780,8 @@
 
             turned_copy(1, 1).wait()
 
-        weight_copy(2, z, slot).wait()
-        tall_copy(z).wait()
+        weight_copy(2, j, slot).wait()
+        tall_copy(j).wait()
 
         @pl.loop(0, 3)
         def _(n):
@@ -752,25 +789,29 @@
             value = (dactive * tall[half, :, tile(n)].astype(F32)).astype(BF)
             dexp[:, tile(n)] = value
             part[pl.ds(10 + z, 1), tile(n)] = jnp.sum(value.astype(F32), axis=0, keepdims=True)
-
-        pl.loop(0, 3)(lambda n: outer(4 + z, 1, dexp, tile(n)))
-        emit(4 + z, 1, z)
-        for k in range(4):
-            pl.when(z == k)(functools.partial(stage, 2 * k + 1))
-        weight_copy(1, z, slot + 1).wait()
+            events("slope", j, n)
+
+        @pl.loop(0, 3)
+        def _(n):
+            outer(4 + j, 1, dexp, tile(n))
+            events("expand", j, n)
+
+        emit(4 + j, 1, z)
+        weight_copy(1, j, slot + 1).wait()
 
         @pl.loop(0, 3)
         def _(n):
             stream[:, tile(n)] = stream[:, tile(n)] + mm(dexp[...], weights[slot + 1, tile(n), :], NT)
-
-        @pl.when(z < 2)
+            events("hidden", j, n)
+
+        @pl.when(j < 2)
         def _():
-            wide_copy(act_in, z + 2).start()
-            tall_copy(z + 2).start()
-            weight_copy(2, z + 2, slot).start()
-            weight_copy(1, z + 2, slot + 1).start()
-
-        @pl.when(z == 2)
+            wide_copy(act_in, j + 2).start()
+            tall_copy(j + 2).start()
+            weight_copy(2, j + 2, slot).start()
+            weight_copy(1, j + 2, slot + 1).start()
+
+        @pl.when(j == 2)
         def _():
             wide_copy(qkv_in, 0).start()
             weight_copy(0, 0, 0).start()
@@ -779,7 +820,7 @@
             ctx_copy(1).start()
             prob_copy(0).start()
 
-        @pl.when(z == 3)
+        @pl.when(j == 3)
         def _():
             wide_copy(qkv_in, 1).start()
             weight_copy(0, 2, 2).start()
@@ -802,28 +843,31 @@
         low[at, :] = dmixed
         turned[1, :, at] = dmixed.T
 
+    events("norm")
     turned_copy(0, 0).wait()
     dproj = tall
     dproj[:, :, 2 * TILE : D] = jnp.zeros((2, tokens, TILE), BF)
 
-    def pull(z):
+    def pull(j):
         @pl.loop(0, 3)
         def _(n):
-            add = mm(dproj[z % 2, :, 0 : 3 * width], weights[z, tile(n), 0 : 3 * width], NT)
+            add = mm(dproj[j % 2, :, 0 : 3 * width], weights[j, tile(n), 0 : 3 * width], NT)
             stream[:, tile(n)] = stream[:, tile(n)] + add
+            events("pull", j, n)
 
     @pl.loop(0, 4)
-    def _(z):
-        half = z % 2
-        weight_copy(0, z, z).wait()
-        wide_copy(qkv_in, z).wait()
-        ctx_copy(z).wait()
-        dctx[...] = mm(low[...], weights[z, :, 3 * width :], NN).astype(BF)
+    def _(j):
+        half = j % 2
+        z = turn_block(j)
+        weight_copy(0, j, j).wait()
+        wide_copy(qkv_in, j).wait()
+        ctx_copy(j).wait()
+        dctx[...] = mm(low[...], weights[j, :, 3 * width :], NN).astype(BF)
 
         @pl.loop(0, rows)
         def _(r):
             at = pl.ds(pl.multiple_of(r * length, 32), length)
-            g = z * rows + r
+            g = j * rows + r
             prob_copy(g).wait()
             pl.when(g + 1 < 4 * rows)(lambda: prob_copy(g + 1).start())
             dq, dk, dv = [], [], []
@@ -846,38 +890,36 @@
             line = pl.ds(6 + z, 1)
             before = jnp.where(r == 0, 0.0, part[line, 0 : 3 * width])
             part[line, 0 : 3 * width] = before + jnp.sum(joined.astype(F32), axis=0, keepdims=True)
+            events("attend", j, r)
 
         if fused:
             for k in range(4):
-                pl.when(z == k)(lambda k=k: scatter.to_core(2 * k).wait_send())
-        pl.loop(0, 3)(lambda n: outer(z, 0, dproj.at[half], tile(n)))
-        outer(z, 1, ctx.at[half], slice(None), slice(3 * width, D), width)
-        emit(z, 0, z)
-        for k in range(4):
-            pl.when(z == k)(functools.partial(stage, 8 + k))
-
-        @pl.when(z < 2)
+                pl.when(j == k)(lambda k=k: scatter.to_core(2 * k).wait_send())
+            pl.when(j == 3)(lambda: scatter.small_stage(part, 0))
+
+        pl.loop(0, 3)(lambda n: outer(j, 0, dproj.at[half], tile(n)))
+        outer(j, 1, ctx.at[half], slice(None), slice(3 * width, D), width)
+        emit(j, 0, z)
+        events("project", j)
+
+        @pl.when(j < 2)
         def _():
-            wide_copy(qkv_in, z + 2).start()
-            ctx_copy(z + 2).start()
-            pull(z)
+            wide_copy(qkv_in, j + 2).start()
+            ctx_copy(j + 2).start()
+            pull(j)
 
     if fused:
-        n = len(Scatter.steps)
-        scatter.small_stage(part, 0)
+        scatter.small_stage(part, 1)
     pull(2)
     if fused:
-        stage(n)
-        scatter.small_stage(part, 1)
+        scatter.small_stage(part, 2)
     pull(3)
     input_copy = pltpu.make_async_copy(stream, input_out, end_sem.at[0])
     input_copy.start()
     if fused:
-        stage(n + 1)
-        scatter.small_stage(part, 2)
+        events("last")
+        scatter.small_stage(part, 3)
         grad_out[2] = scatter.total(2)
-        scatter.small_stage(part, 3)
-        stage(n + 2)
         grad_out[1] = scatter.total(1)
         small_out[...] = scatter.small_stage(part, 4)
         grad_out[0] = scatter.total(0)

time: 228 us -> 215 us (0.943); the launches traced: 224 us -> 215 us
  Pallas kernels: 223 us -> 214 us
    pallas_call x1, Pallas kernels: 103 us -> 88 us  [run_forward(): pl.pallas_call(functools.partial(forward_kernel, fused, rows, length), ou...]
    pallas_call x1, Pallas kernels: 112 us -> 118 us  [run_backward(): pl.pallas_call(functools.partial(backward_kernel, fused, rows, length), o...]
where the time goes in v1:
time: 215 us
  Pallas kernels  214 us (100%)
    pallas_call x1, Pallas kernels, run_backward(): pl.pallas_call(functools.partial(backward_kernel, fused, rows, length), o...  118 us
    pallas_call x1, Pallas kernels, run_forward(): pl.pallas_call(functools.partial(forward_kernel, fused, rows, length), ou...  88 us
    pallas_call x1, Pallas kernels, update_all(): pl.pallas_call(update_kernel, out_shape=tuple(shapes + kept), in_specs=[v...  8.5 us

profile of v1, /device:TPU:0, one launch (start us, length us, event | category | flops | bytes accessed | tf_op | source)
XLA Modules:
  0.0 215.1 jit_solution(1625368984021192521)
XLA Ops:
  0.7 88.0 %forward.1 = (bf16[3,4,4,2,96,768]{5,4,3,2,1,0:T(8,128)(2,1)}, bf16[4,1152,768]{2,1,0:T(8,128)(2,1)}, bf16[4,1152,192]{2,1,0:T(8,128)(2,1)}, bf16[4,4,3,288,288]...) custom-call(bf16[1152,768]{1,0:T(8,128)(2,1)} %bitcast.31, ...), custom_call_target="tpu_custom_call" | custom-call | tf_op jit(solution)/shard_map/forward/pallas_call | solution.py:611
  88.7 117.7 %backward.1 = (f32[3,96,768]{2,1,0:T(8,128)}, f32[16,768]{1,0:T(8,128)}, f32[1152,768]{1,0:T(8,128)}) custom-call(bf16[6,768]{1,0:T(8,128)(2,1)} %refs_0_.2, f32[8,768]{1,0:T(8,128)} %get-tuple-element.75.refs_1_, bf16[3,4,768,768]{3,2,1,0:T(8,128)(2,1)} %bitcast.30, bf16[4,1152,768]{2,1,0:T(8,128)(2,1)} %get-tuple-element.77.refs_3_, ...), custom_call_target="tpu_custom_call" | custom-call | tf_op jit(solution)/shard_map/backward/pallas_call | solution.py:943
  206.5 8.5 %update.1 = (f32[3,96,192]{2,1,0:T(8,128)}, f32[3,96,192]{2,1,0:T(8,128)}, f32[3,96,192]{2,1,0:T(8,128)}, bf16[3,96,192]{2,1,0:T(8,128)(2,1)}, f32[3,2,8]{2,1,0:...) custom-call(f32[3,96,768]{2,1,0:T(8,128)} %get-tuple-element.86.redu, ...), custom_call_target="tpu_custom_call" | custom-call | tf_op jit(solution)/shard_map/update/pallas_call | solution.py:1047

commit v2 on v1

--- a/solution.py
+++ b/solution.py
@@ -74,8 +74,12 @@
     pl.semaphore_wait(barrier, 6)
 
 
+def crossed(z, d):
+    return (z // 2 + d // 2) % 2 * 2 + (z % 2 + d % 2) % 2
+
+
 class Gather:
-    steps = [(0, 1), (0, 2), (0, 3), (1, 1), (2, 1), (1, 2), (2, 2), (1, 3), (2, 3)]
+    steps = [(1, 1), (0, 1), (0, 2), (0, 3), (2, 1), (1, 2), (2, 2), (1, 3), (2, 3)]
     sems = [(3,)] + [(3, 3)] * 12 + [(3,)] * 2
 
     def __init__(self, mats, whole, bias, biases, sems):
@@ -90,17 +94,17 @@
 
     def small(self, d):
         p, z = self.where[:2]
-        return remote(self.bias, self.biases.at[z], self.ss.at[d - 1], self.sr.at[d - 1], p, (z + d) % 4)
+        return remote(self.bias, self.biases.at[z], self.ss.at[d - 1], self.sr.at[d - 1], p, crossed(z, d))
 
     def along_z(self, m, d):
         p, z, core, xy = self.where[:4]
         own = self.whole.at[m, z] if m == 0 else self.mats[m - 1]
         return remote(own.at[xy, core], self.whole.at[m, z, xy, core], self.zs.at[m, d - 1],
-                      self.zr.at[m, d - 1], p, (z + d) % 4)
+                      self.zr.at[m, d - 1], p, crossed(z, d))
 
     def plane(self, m, d, block, rows, send_sem, recv_sem, peer):
         z = self.where[1]
-        part = self.whole.at[m, (z + 4 - d) % 4, block, self.where[2], rows]
+        part = self.whole.at[m, crossed(z, d), block, self.where[2], rows]
         return remote(part, part, send_sem.at[m, d - 1], recv_sem.at[m, d - 1], peer, z)
 
     def to_x(self, m, d):
@@ -117,12 +121,15 @@
 
     def to_core(self, m, d):
         z = self.where[1]
-        part = self.whole.at[m, (z + 4 - d) % 4, :, self.where[2]]
+        part = self.whole.at[m, crossed(z, d), :, self.where[2]]
         return remote(part, part, self.cs.at[m, d - 1], self.cr.at[m, d - 1], self.where[4], z)
 
     def begin(self):
         p, z, _, _, pc, px, py = self.where[:7]
         greet(p, z, pc, px, py)
+        self.along_z(1, 1).start()
+
+    def begin_first(self):
         for d in (1, 2, 3):
             self.along_z(0, d).start()
             self.small(d).start()
@@ -131,11 +138,11 @@
         m, d = self.steps[i]
         if kind == 0:
             self.along_z(m, d).wait_recv()
-            if i < 3:
+            if m == 0:
                 self.small(d).wait_recv()
             self.to_x(m, d).start()
             self.to_y(m, d).start()
-            if m < 2:
+            if m < 2 and (m, d) != (0, 1):
                 self.along_z(m + 1, d).start()
         elif kind == 1:
             self.to_x(m, d).wait_recv()
@@ -312,22 +319,26 @@
 NN = ((1,), (0,))
 CHUNK = 384
 STRIP = 128
-TILE = 256
 VMEM_MOST = 60 << 20
 EVENTS = {
-    "block": {(1, 0): ((1, 0), (0, 1), (2, 0), (0, 2), (3, 0)), (2, 0): ((0, 5), (1, 3), (3, 1)), (3, 0): ((2, 3),)},
-    "project": {(1, 2): ((1, 1),)},
-    "attend": {(0, 3): ((0, 0),), (1, 0): ((0, 3),), (1, 2): ((1, 2),), (1, 3): ((2, 1),), (2, 0): ((2, 2), (0, 7)), (2, 3): ((1, 5), (0, 4), (3, 2)), (3, 1): ((1, 7), (3, 3)), (3, 2): ((2, 5), (0, 6))},
-    "turn": {},
-    "norm": {(0, 0): ((1, 4), (0, 8), (3, 5), (2, 7))},
-    "feed": {(1, 0): ((1, 8), (3, 4)), (2, 0): ((3, 6),)},
-    "expand": {(0, 2): ((1, 6),), (1, 2): ((2, 6),), (2, 2): ((3, 8),)},
-    "shrink": {(0, 1): ((3, 7),), (0, 2): ((2, 4),), (1, 1): ((2, 8),)},
+    "block": {(1, 0): ((0, 2), (1, 0), (0, 4), (1, 1), (0, 3), (1, 2), (2, 0), (3, 0), (1, 4), (0, 5), (2, 1), (3, 1)), (2, 0): ((3, 2),), (3, 0): ((1, 7), (3, 3))},
+    "project": {(1, 1): ((1, 3),), (2, 1): ((1, 5),), (3, 1): ((2, 5),)},
+    "attend": {(0, 1): ((0, 0),), (1, 1): ((2, 2),), (1, 2): ((0, 7), (2, 4)), (2, 0): ((3, 4),), (2, 1): ((2, 3),), (2, 2): ((0, 6),), (3, 2): ((0, 8), (1, 6)), (3, 3): ((3, 5),)},
+    "turn": {(0, 0): ((0, 1),)},
+    "norm": {(0, 0): ((2, 7),)},
+    "feed": {},
+    "middle": {},
+    "expand": {(0, 0): ((3, 7), (1, 8)), (0, 1): ((2, 6),), (1, 0): ((2, 8),), (1, 1): ((3, 6),), (2, 0): ((3, 8),)},
+    "shrink": {},
 }
 
 
-def tile(n):
-    return pl.ds(pl.multiple_of(n * TILE, TILE), TILE)
+def half(n, tokens):
+    return pl.ds(pl.multiple_of(n * (tokens // 2), 32), tokens // 2)
+
+
+def square(whole, m, z):
+    return whole[m, z].reshape(D, D)
 
 
 def strip(s):
@@ -362,6 +373,7 @@
         for copy in joint_copies:
             copy.start()
         gather = Gather((e_ref, s_ref), whole, bias, biases, gather_sems)
+        gather.begin()
         bias[...] = jnp.zeros_like(bias)
         for h in range(heads):
             for j in (0, 1):
@@ -372,9 +384,9 @@
         for copy in joint_copies:
             copy.wait()
         for j in (0, 1):
-            half = joint[:, j * CHUNK : (j + 1) * CHUNK].T
-            whole[0, z_own, 2 * j : 2 * j + 2] = half.reshape(2, 2, SLICE, D)
-        gather.begin()
+            columns = joint[:, j * CHUNK : (j + 1) * CHUNK].T
+            whole[0, z_own, 2 * j : 2 * j + 2] = columns.reshape(2, 2, SLICE, D)
+        gather.begin_first()
         gather.local(1).start()
         gather.local(2).start()
         own_bias = pltpu.make_async_copy(bias, biases.at[z_own], w_sem.at[0])
@@ -391,10 +403,7 @@
     vec[0:6, :] = vec_in[...].astype(F32)
 
     def block(i):
-        return (z_own + 3 * i) % 4
-
-    def columns(m, z, n):
-        return whole[m, z, :, :, :, tile(n)].reshape(D, TILE)
+        return crossed(z_own, i)
 
     def turned_copy(slot):
         return pltpu.make_async_copy(turned.at[slot], turned_out.at[slot], end_sem.at[slot])
@@ -438,10 +447,10 @@
             qkv_copy(i - 2).wait()
             ctx_copy(i - 2).wait()
 
-        @pl.loop(0, 3)
+        @pl.loop(0, 2)
         def _(n):
-            add = biases[z, 0:1, tile(n)]
-            qkv[slot, :, tile(n)] = (mm(x[...], columns(0, z, n), NN) + add).astype(BF)
+            at = half(n, tokens)
+            qkv[slot, at, :] = (mm(x[at, :], square(whole, 0, z), NN) + biases[z, 0:1, :]).astype(BF)
             events("project", i, n)
 
         qkv_copy(i).start()
@@ -454,18 +463,21 @@
             number = lax.broadcasted_iota(jnp.int32, (8, length), 0)
             among = jnp.where(number == pair, 1.0, 0.0).astype(BF)
             mask = (mm(among, among, TN) - 1.0) * -MASKED
-            done = []
+
+            def part_of(j, h):
+                return qkv[slot, at, j * width + h * HEAD : j * width + (h + 1) * HEAD]
+
+            scale = jnp.asarray(HEAD ** (-0.5), BF)
+            scores = [mm(part_of(1, h), part_of(0, h) * scale, NT) + mask for h in range(heads)]
+            probs = []
             for h in range(heads):
-                q = qkv[slot, at, h * HEAD : (h + 1) * HEAD] * jnp.asarray(HEAD ** (-0.5), BF)
-                k = qkv[slot, at, width + h * HEAD : width + (h + 1) * HEAD]
-                v = qkv[slot, at, 2 * width + h * HEAD : 2 * width + (h + 1) * HEAD]
-                scores = mm(k, q, NT) + mask
-                weights = jnp.exp(scores - jnp.max(scores, axis=0, keepdims=True))
+                weights = jnp.exp(scores[h] - jnp.max(scores[h], axis=0, keepdims=True))
                 share = 1.0 / jnp.sum(weights, axis=0, keepdims=True)
-                probs = (weights * share).astype(BF)
-                prob[r, h] = probs
-                done.append(mm(v, probs, TN).astype(BF).T)
-            ctx[slot, at, :] = jnp.concatenate(done, axis=1)
+                probs.append((weights * share).astype(BF))
+            for h in range(heads):
+                prob[r, h] = probs[h]
+            done = [mm(part_of(2, h), probs[h], TN).astype(BF) for h in range(heads)]
+            ctx[slot, at, :] = jnp.concatenate(done, axis=0).T
             prob_copy(i, r).start()
             events("attend", i, r)
 
@@ -485,7 +497,7 @@
         @pl.loop(0, tokens // CHUNK)
         def _(c):
             at = pl.ds(pl.multiple_of(c * CHUNK, CHUNK), CHUNK)
-            add = mm(ctx[slot, at, :], whole[0, z].reshape(D, D)[:, 3 * width :], NT)
+            add = mm(ctx[slot, at, :], square(whole, 0, z)[:, 3 * width :], NT)
             mixed[at, :] = mixed[at, :] + add
 
     whole_copy(0).start()
@@ -522,20 +534,23 @@
             act_copy(i - 2).wait()
             slope_copy(i - 2).wait()
 
-        @pl.loop(0, 3)
+        @pl.loop(0, 2)
         def _(n):
-            u = mm(low[...], columns(1, z, n), NN) + biases[z, 1:2, tile(n)]
+            at = half(n, tokens)
+            u = mm(low[at, :], square(whole, 1, z), NN) + biases[z, 1:2, :]
             cumulative = 0.5 + 0.5 * lax.erf(u * SQRT_HALF)
-            act[slot, :, tile(n)] = (u * cumulative).astype(BF)
-            slope[slot, :, tile(n)] = (cumulative + u * jnp.exp(-0.5 * u * u) * INV_ROOT_TAU).astype(BF)
+            act[slot, at, :] = (u * cumulative).astype(BF)
+            slope[slot, at, :] = (cumulative + u * jnp.exp(-0.5 * u * u) * INV_ROOT_TAU).astype(BF)
             events("expand", i, n)
 
         act_copy(i).start()
         slope_copy(i).start()
-
-        @pl.loop(0, 3)
+        events("middle", i)
+
+        @pl.loop(0, 2)
         def _(n):
-            mixed[:, tile(n)] = mixed[:, tile(n)] + mm(act[slot], columns(2, z, n), NN)
+            at = half(n, tokens)
+            mixed[at, :] = mixed[at, :] + mm(act[slot, at, :], square(whole, 2, z), NN)
             events("shrink", i, n)
 
         @pl.when(i == 2)
@@ -559,15 +574,19 @@
         part[3:4, :] += jnp.sum(back * normal, axis=0, keepdims=True)
         part[4:5, :] += jnp.sum(back, axis=0, keepdims=True)
         part[5:6, :] += jnp.sum(dsummed, axis=0, keepdims=True)
+        pltpu.make_async_copy(normed.at[at], ds_out.at[at], end_sem.at[5]).start()
+        pltpu.make_async_copy(result.at[at], result_out.at[at], end_sem.at[6]).start()
 
     last = [
         turned_copy(2),
-        pltpu.make_async_copy(normed, ds_out, end_sem.at[5]),
-        pltpu.make_async_copy(result, result_out, end_sem.at[6]),
         pltpu.make_async_copy(part, part_out, end_sem.at[7]),
     ]
     for copy in last:
         copy.start()
+    last = last + [
+        pltpu.make_async_copy(normed, ds_out, end_sem.at[5]),
+        pltpu.make_async_copy(result, result_out, end_sem.at[6]),
+    ]
     for i in (2, 3):
         qkv_copy(i).wait()
         ctx_copy(i).wait()
@@ -664,15 +683,15 @@
 
 
 BACK_EVENTS = {
-    "shrink": {(0, 2): ((0, 0),), (1, 2): ((0, 2),), (2, 2): ((0, 4),), (3, 1): ((3, 1),), (3, 2): ((0, 6),)},
-    "slope": {(1, 1): ((1, 1),), (2, 0): ((2, 1), (1, 3)), (2, 2): ((3, 0),), (3, 0): ((1, 5),), (3, 2): ((2, 3),)},
-    "expand": {(0, 2): ((0, 1), (1, 0)), (1, 1): ((2, 0),), (1, 2): ((0, 3), (1, 2)), (2, 2): ((0, 5), (1, 4)), (3, 2): ((0, 7), (1, 6))},
-    "hidden": {(2, 1): ((2, 2),), (3, 2): ((2, 4),)},
-    "norm": {(0, 0): ((3, 2), (1, 7))},
-    "attend": {(0, 0): ((2, 5),), (0, 1): ((3, 3),), (1, 1): ((2, 7), (1, 8)), (1, 2): ((3, 5),), (2, 1): ((2, 8), (1, 9)), (3, 2): ((2, 9),), (3, 3): ((1, 10),)},
-    "project": {(0, 0): ((0, 8), (2, 6)), (1, 0): ((0, 9), (3, 6), (3, 7)), (2, 0): ((0, 10), (3, 8)), (3, 0): ((0, 11),)},
-    "pull": {(0, 1): ((3, 4),), (2, 2): ((3, 9),)},
-    "last": {(0, 0): ((1, 11), (2, 10), (2, 11), (3, 10), (3, 11))},
+    "shrink": {(0, 0): ((0, 0),), (1, 0): ((0, 2),), (2, 0): ((0, 4), (2, 1), (1, 3)), (3, 0): ((0, 6), (1, 5))},
+    "slope": {(1, 0): ((1, 1),), (1, 1): ((2, 0),), (2, 0): ((3, 0),), (3, 0): ((2, 3),)},
+    "expand": {(0, 0): ((0, 1), (1, 0)), (1, 0): ((0, 3), (1, 2)), (2, 0): ((0, 5), (1, 4), (2, 2)), (3, 0): ((0, 7), (1, 6), (2, 4))},
+    "hidden": {(2, 0): ((3, 1),), (3, 1): ((3, 2),)},
+    "norm": {(0, 0): ((1, 7), (2, 5))},
+    "attend": {(0, 0): ((3, 3),), (0, 2): ((2, 6),), (0, 3): ((3, 4),), (1, 0): ((3, 5),), (1, 1): ((1, 8), (3, 6)), (1, 2): ((3, 7),), (2, 1): ((1, 9), (3, 8)), (3, 0): ((2, 9),), (3, 2): ((1, 10),), (3, 3): ((3, 9),)},
+    "project": {(0, 0): ((0, 8),), (1, 0): ((0, 9),), (2, 0): ((0, 10),), (3, 0): ((0, 11),)},
+    "pull": {(0, 0): ((2, 7),), (1, 0): ((2, 8),), (3, 0): ((2, 10),)},
+    "last": {(0, 0): ((1, 11), (3, 10), (2, 11), (3, 11))},
 }
 
 
@@ -744,9 +763,10 @@
     part[...] = jnp.zeros_like(part)
     part[0:VECTORS, :] = part_in[...]
 
-    def outer(slot, turned_slot, right, lanes, offset=0, size=TILE):
-        product = mm(turned[turned_slot], right[:, lanes], NN).astype(BF)
-        grads[slot, :, :, :, offset if size != TILE else lanes] = product.reshape(4, 2, SLICE, size)
+    def outer(slot, turned_slot, right, offset=0):
+        product = mm(turned[turned_slot], right, NN).astype(BF)
+        count = product.shape[1]
+        grads[slot, :, :, :, offset : offset + count] = product.reshape(4, 2, SLICE, count)
 
     def emit(slot, m, z):
         if not fused:
@@ -758,16 +778,13 @@
 
     @pl.loop(0, 4)
     def _(j):
-        half = j % 2
-        slot = 2 * half
+        parity = j % 2
+        slot = 2 * parity
         z = turn_block(j)
         wide_copy(act_in, j).wait()
 
-        @pl.loop(0, 3)
-        def _(n):
-            outer(j, 0, wide.at[half], tile(n))
-            events("shrink", j, n)
-
+        outer(j, 0, wide[parity])
+        events("shrink", j)
         emit(j, 2, z)
 
         @pl.when(j == 0)
@@ -783,25 +800,25 @@
         weight_copy(2, j, slot).wait()
         tall_copy(j).wait()
 
-        @pl.loop(0, 3)
+        @pl.loop(0, 2)
         def _(n):
-            dactive = mm(low[...], weights[slot, tile(n), :], NT)
-            value = (dactive * tall[half, :, tile(n)].astype(F32)).astype(BF)
-            dexp[:, tile(n)] = value
-            part[pl.ds(10 + z, 1), tile(n)] = jnp.sum(value.astype(F32), axis=0, keepdims=True)
+            at = half(n, tokens)
+            dactive = mm(low[at, :], weights[slot], NT)
+            value = (dactive * tall[parity, at, :].astype(F32)).astype(BF)
+            dexp[at, :] = value
+            line = pl.ds(10 + z, 1)
+            part[line, :] = part[line, :] + jnp.sum(value.astype(F32), axis=0, keepdims=True)
             events("slope", j, n)
 
-        @pl.loop(0, 3)
-        def _(n):
-            outer(4 + j, 1, dexp, tile(n))
-            events("expand", j, n)
-
+        outer(4 + j, 1, dexp[...])
+        events("expand", j)
         emit(4 + j, 1, z)
         weight_copy(1, j, slot + 1).wait()
 
-        @pl.loop(0, 3)
+        @pl.loop(0, 2)
         def _(n):
-            stream[:, tile(n)] = stream[:, tile(n)] + mm(dexp[...], weights[slot + 1, tile(n), :], NT)
+            at = half(n, tokens)
+            stream[at, :] = stream[at, :] + mm(dexp[at, :], weights[slot + 1], NT)
             events("hidden", j, n)
 
         @pl.when(j < 2)
@@ -846,18 +863,17 @@
     events("norm")
     turned_copy(0, 0).wait()
     dproj = tall
-    dproj[:, :, 2 * TILE : D] = jnp.zeros((2, tokens, TILE), BF)
 
     def pull(j):
-        @pl.loop(0, 3)
+        @pl.loop(0, 2)
         def _(n):
-            add = mm(dproj[j % 2, :, 0 : 3 * width], weights[j, tile(n), 0 : 3 * width], NT)
-            stream[:, tile(n)] = stream[:, tile(n)] + add
+            at = half(n, tokens)
+            stream[at, :] = stream[at, :] + mm(dproj[j % 2, at, 0 : 3 * width], weights[j, :, 0 : 3 * width], NT)
             events("pull", j, n)
 
     @pl.loop(0, 4)
     def _(j):
-        half = j % 2
+        parity = j % 2
         z = turn_block(j)
         weight_copy(0, j, j).wait()
         wide_copy(qkv_in, j).wait()
@@ -870,23 +886,26 @@
             g = j * rows + r
             prob_copy(g).wait()
             pl.when(g + 1 < 4 * rows)(lambda: prob_copy(g + 1).start())
-            dq, dk, dv = [], [], []
             scale = jnp.asarray(HEAD ** (-0.5), BF)
+
+            def part_of(i, h):
+                return wide[parity, at, i * width + h * HEAD : i * width + (h + 1) * HEAD]
+
+            def dc(h):
+                return dctx[at, h * HEAD : (h + 1) * HEAD]
+
+            dprobs = [mm(part_of(2, h), dc(h), NT) for h in range(heads)]
+            dscores = []
             for h in range(heads):
-                q = wide[half, at, h * HEAD : (h + 1) * HEAD] * scale
-                k = wide[half, at, width + h * HEAD : width + (h + 1) * HEAD]
-                v = wide[half, at, 2 * width + h * HEAD : 2 * width + (h + 1) * HEAD]
-                dc = dctx[at, h * HEAD : (h + 1) * HEAD]
-                probs = prob[g % 2, h]
-                full = probs.astype(F32)
-                dprobs = mm(v, dc, NT)
-                inner = jnp.sum(full * dprobs, axis=0, keepdims=True)
-                dscores = (full * (dprobs - inner)).astype(BF)
-                dv.append(mm(probs, dc, NN).astype(BF))
-                dk.append(mm(dscores, q, NN).astype(BF))
-                dq.append((mm(k, dscores, TN) * HEAD ** (-0.5)).astype(BF).T)
+                full = prob[g % 2, h].astype(F32)
+                inner = jnp.sum(full * dprobs[h], axis=0, keepdims=True)
+                dscores.append((full * (dprobs[h] - inner)).astype(BF))
+            dv = [mm(prob[g % 2, h], dc(h), NN).astype(BF) for h in range(heads)]
+            dk = [mm(dscores[h], part_of(0, h) * scale, NN).astype(BF) for h in range(heads)]
+            dq = [(mm(part_of(1, h), dscores[h], TN) * HEAD ** (-0.5)).astype(BF) for h in range(heads)]
+            dq = [jnp.concatenate(dq, axis=0).T]
             joined = jnp.concatenate(dq + dk + dv, axis=1)
-            dproj[half, at, 0 : 3 * width] = joined
+            dproj[parity, at, 0 : 3 * width] = joined
             line = pl.ds(6 + z, 1)
             before = jnp.where(r == 0, 0.0, part[line, 0 : 3 * width])
             part[line, 0 : 3 * width] = before + jnp.sum(joined.astype(F32), axis=0, keepdims=True)
@@ -897,8 +916,8 @@
                 pl.when(j == k)(lambda k=k: scatter.to_core(2 * k).wait_send())
             pl.when(j == 3)(lambda: scatter.small_stage(part, 0))
 
-        pl.loop(0, 3)(lambda n: outer(j, 0, dproj.at[half], tile(n)))
-        outer(j, 1, ctx.at[half], slice(None), slice(3 * width, D), width)
+        outer(j, 0, dproj[parity, :, 0 : 3 * width])
+        outer(j, 1, ctx[parity], 3 * width)
         emit(j, 0, z)
         events("project", j)
 

time: 215 us -> 197 us (0.916)
  Pallas kernels: 214 us -> 195 us
    pallas_call x1, Pallas kernels: 118 us -> 99.2 us  [run_backward(): pl.pallas_call(functools.partial(backward_kernel, fused, rows, length), o...]
where the time goes in v2:
time: 197 us; the launch traced here: 196 us
  Pallas kernels  195 us (99%)
    pallas_call x1, Pallas kernels, run_backward(): pl.pallas_call(functools.partial(backward_kernel, fused, rows, length), o...  99.2 us
    pallas_call x1, Pallas kernels, run_forward(): pl.pallas_call(functools.partial(forward_kernel, fused, rows, length), ou...  87.6 us
    pallas_call x1, Pallas kernels, update_all(): pl.pallas_call(update_kernel, out_shape=tuple(shapes + kept), in_specs=[v...  8.5 us

profile of v2, /device:TPU:0, one launch (start us, length us, event | category | flops | bytes accessed | tf_op | source)
XLA Modules:
  0.0 196.1 jit_solution(2028557835806989588)
XLA Ops:
  0.7 87.6 %forward.1 = (bf16[3,4,4,2,96,768]{5,4,3,2,1,0:T(8,128)(2,1)}, bf16[4,1152,768]{2,1,0:T(8,128)(2,1)}, bf16[4,1152,192]{2,1,0:T(8,128)(2,1)}, bf16[4,4,3,288,288]...) custom-call(bf16[1152,768]{1,0:T(8,128)(2,1)} %bitcast.31, ...), custom_call_target="tpu_custom_call" | custom-call | tf_op jit(solution)/shard_map/forward/pallas_call | solution.py:630
  88.2 99.2 %backward.1 = (f32[3,96,768]{2,1,0:T(8,128)}, f32[16,768]{1,0:T(8,128)}, f32[1152,768]{1,0:T(8,128)}) custom-call(bf16[6,768]{1,0:T(8,128)(2,1)} %refs_0_.2, f32[8,768]{1,0:T(8,128)} %get-tuple-element.75.refs_1_, bf16[3,4,768,768]{3,2,1,0:T(8,128)(2,1)} %bitcast.30, bf16[4,1152,768]{2,1,0:T(8,128)(2,1)} %get-tuple-element.77.refs_3_, ...), custom_call_target="tpu_custom_call" | custom-call | tf_op jit(solution)/shard_map/backward/pallas_call | solution.py:962
  187.4 8.5 %update.1 = (f32[3,96,192]{2,1,0:T(8,128)}, f32[3,96,192]{2,1,0:T(8,128)}, f32[3,96,192]{2,1,0:T(8,128)}, bf16[3,96,192]{2,1,0:T(8,128)(2,1)}, f32[3,2,8]{2,1,0:...) custom-call(f32[3,96,768]{2,1,0:T(8,128)} %get-tuple-element.86.redu, ...), custom_call_target="tpu_custom_call" | custom-call | tf_op jit(solution)/shard_map/update/pallas_call | solution.py:1066

commit v3 on v2

--- a/solution.py
+++ b/solution.py
@@ -221,8 +221,7 @@
 
             @pl.loop(0, 4)
             def _(q):
-                mine = self.grads[self.slots[j], q, core].astype(F32)
-                self.sum[j, q] = (self.sum[j, q].astype(F32) + mine).astype(BF)
+                self.sum[j, q] = self.sum[j, q] + self.grads[self.slots[j], q, core]
 
             for t in (1, 0):
                 self.to_x(j, t).start()
@@ -321,14 +320,14 @@
 STRIP = 128
 VMEM_MOST = 60 << 20
 EVENTS = {
-    "block": {(1, 0): ((0, 2), (1, 0), (0, 4), (1, 1), (0, 3), (1, 2), (2, 0), (3, 0), (1, 4), (0, 5), (2, 1), (3, 1)), (2, 0): ((3, 2),), (3, 0): ((1, 7), (3, 3))},
-    "project": {(1, 1): ((1, 3),), (2, 1): ((1, 5),), (3, 1): ((2, 5),)},
-    "attend": {(0, 1): ((0, 0),), (1, 1): ((2, 2),), (1, 2): ((0, 7), (2, 4)), (2, 0): ((3, 4),), (2, 1): ((2, 3),), (2, 2): ((0, 6),), (3, 2): ((0, 8), (1, 6)), (3, 3): ((3, 5),)},
+    "block": {(1, 0): ((1, 0), (1, 1), (0, 2), (2, 0), (0, 3), (3, 0), (2, 1), (1, 2), (3, 1)), (2, 0): ((2, 3), (3, 2))},
+    "project": {},
+    "attend": {(0, 1): ((0, 0),), (1, 1): ((1, 3), (0, 5)), (1, 2): ((2, 2), (0, 4)), (2, 0): ((0, 7), (3, 3)), (2, 1): ((1, 5),), (3, 0): ((0, 6),), (3, 1): ((1, 7), (1, 4)), (3, 2): ((2, 5),)},
     "turn": {(0, 0): ((0, 1),)},
-    "norm": {(0, 0): ((2, 7),)},
+    "norm": {(0, 0): ((3, 5), (1, 6), (0, 8))},
     "feed": {},
     "middle": {},
-    "expand": {(0, 0): ((3, 7), (1, 8)), (0, 1): ((2, 6),), (1, 0): ((2, 8),), (1, 1): ((3, 6),), (2, 0): ((3, 8),)},
+    "expand": {(0, 0): ((2, 7),), (0, 1): ((2, 4),), (1, 0): ((3, 7),), (1, 1): ((3, 4), (1, 8), (2, 6)), (2, 1): ((3, 6), (2, 8)), (3, 1): ((3, 8),)},
     "shrink": {},
 }
 
@@ -350,10 +349,10 @@
     x_in, cot_in, seg_ref, vec_in = refs[:4]
     n_in = 10 if fused else 6
     ins = refs[4:n_in]
-    outs = refs[n_in : n_in + 12]
-    (whole_out, qkv_out, ctx_out, prob_out, act_out, slope_out, normed_out, rstd_out, ds_out, turned_out, result_out,
-     part_out) = outs
-    rest = refs[n_in + 12 :]
+    outs = refs[n_in : n_in + 13]
+    (whole_out, qkv_out, ctx_out, prob_out, act_out, slope_out, normed_out, rstd_out, ds_out, turned_out, low_out,
+     result_out, part_out) = outs
+    rest = refs[n_in + 13 :]
     gather_sems, rest = rest[:n_sem], rest[n_sem:]
     (whole, bias, biases, joint, vec, x, cot, qkv, ctx, prob, act, slope, mixed, normed, rstd, low, turned,
      result, part, in_sem, w_sem, qkv_sem, ctx_sem, prob_sem, act_sem, slope_sem, end_sem) = rest
@@ -546,17 +545,14 @@
         act_copy(i).start()
         slope_copy(i).start()
         events("middle", i)
+        for m in (1, 2):
+            pltpu.make_async_copy(whole.at[m, z], whole_out.at[m, z], w_sem.at[m]).start()
 
         @pl.loop(0, 2)
         def _(n):
             at = half(n, tokens)
             mixed[at, :] = mixed[at, :] + mm(act[slot, at, :], square(whole, 2, z), NN)
             events("shrink", i, n)
-
-        @pl.when(i == 2)
-        def _():
-            whole_copy(1).start()
-            whole_copy(2).start()
 
     normed_copy.wait()
     cot_copy.wait()
@@ -570,12 +566,15 @@
         back = cot[at, :].astype(F32)
         dsummed = norm_backward(back, vec[3:4, :], normal, scale)
         normed[at, :] = dsummed
-        turned[2, :, at] = dsummed.astype(BF).T
+        dsummed_low = dsummed.astype(BF)
+        low[at, :] = dsummed_low
+        turned[2, :, at] = dsummed_low.T
         part[3:4, :] += jnp.sum(back * normal, axis=0, keepdims=True)
         part[4:5, :] += jnp.sum(back, axis=0, keepdims=True)
         part[5:6, :] += jnp.sum(dsummed, axis=0, keepdims=True)
         pltpu.make_async_copy(normed.at[at], ds_out.at[at], end_sem.at[5]).start()
         pltpu.make_async_copy(result.at[at], result_out.at[at], end_sem.at[6]).start()
+        pltpu.make_async_copy(low.at[at], low_out.at[at], end_sem.at[8]).start()
 
     last = [
         turned_copy(2),
@@ -586,6 +585,7 @@
     last = last + [
         pltpu.make_async_copy(normed, ds_out, end_sem.at[5]),
         pltpu.make_async_copy(result, result_out, end_sem.at[6]),
+        pltpu.make_async_copy(low, low_out, end_sem.at[8]),
     ]
     for i in (2, 3):
         qkv_copy(i).wait()
@@ -641,10 +641,11 @@
             shape(flat, F32),
             shape((3, D, tokens), BF),
             shape(flat, BF),
+            shape(flat, BF),
             shape((VECTORS, D), F32),
         ),
         in_specs=[hbm, hbm, vmem, vmem] + spaces,
-        out_specs=(hbm,) * 12,
+        out_specs=(hbm,) * 13,
         scratch_shapes=([dma(s) for s in Gather.sems] if fused else [])
         + [
             pltpu.VMEM((3, 4) + block, BF),
@@ -673,7 +674,7 @@
             dma((rows,)),
             dma((2,)),
             dma((2,)),
-            dma((8,)),
+            dma((9,)),
         ],
         compiler_params=pltpu.CompilerParams(
             collective_id=0 if fused else None, has_side_effects=True, vmem_limit_bytes=VMEM_MOST
@@ -688,10 +689,10 @@
     "expand": {(0, 0): ((0, 1), (1, 0)), (1, 0): ((0, 3), (1, 2)), (2, 0): ((0, 5), (1, 4), (2, 2)), (3, 0): ((0, 7), (1, 6), (2, 4))},
     "hidden": {(2, 0): ((3, 1),), (3, 1): ((3, 2),)},
     "norm": {(0, 0): ((1, 7), (2, 5))},
-    "attend": {(0, 0): ((3, 3),), (0, 2): ((2, 6),), (0, 3): ((3, 4),), (1, 0): ((3, 5),), (1, 1): ((1, 8), (3, 6)), (1, 2): ((3, 7),), (2, 1): ((1, 9), (3, 8)), (3, 0): ((2, 9),), (3, 2): ((1, 10),), (3, 3): ((3, 9),)},
-    "project": {(0, 0): ((0, 8),), (1, 0): ((0, 9),), (2, 0): ((0, 10),), (3, 0): ((0, 11),)},
-    "pull": {(0, 0): ((2, 7),), (1, 0): ((2, 8),), (3, 0): ((2, 10),)},
-    "last": {(0, 0): ((1, 11), (3, 10), (2, 11), (3, 11))},
+    "attend": {(0, 0): ((3, 3),), (0, 2): ((2, 6),), (0, 3): ((3, 4),), (1, 0): ((3, 5),), (1, 1): ((1, 8), (3, 6)), (1, 2): ((3, 7),), (2, 0): ((2, 8),), (2, 2): ((1, 9),), (2, 3): ((3, 8),), (3, 1): ((2, 9),), (3, 2): ((1, 10),)},
+    "project": {(0, 0): ((0, 8),), (1, 0): ((0, 9),), (2, 0): ((0, 10),), (3, 0): ((0, 11), (3, 9))},
+    "pull": {(0, 0): ((2, 7),), (2, 0): ((2, 10),), (3, 0): ((1, 11),)},
+    "last": {(0, 0): ((3, 10), (2, 11), (3, 11))},
 }
 
 
@@ -702,11 +703,12 @@
 def backward_kernel(fused, rows, length, *refs):
     n_sem = len(Scatter.sems) if fused else 0
     n_buf = len(Scatter.buffers) if fused else 0
-    (vec_in, part_in, whole, qkv_in, ctx_in, prob_in, act_in, slope_in, normed_in, rstd_in, ds_in, turned_in) = refs[:12]
-    grad_out, small_out, input_out = refs[12:15]
-    rest = refs[15:]
+    (vec_in, part_in, whole, qkv_in, ctx_in, prob_in, act_in, slope_in, normed_in, rstd_in, ds_in, turned_in,
+     low_in) = refs[:13]
+    grad_out, small_out, input_out = refs[13:16]
+    rest = refs[16:]
     buffers, sems, rest = rest[:n_buf], rest[n_buf : n_buf + n_sem], rest[n_buf + n_sem :]
-    (grads, weights, wide, tall, dexp, stream, normed, rstd, low, turned, prob, ctx, dctx, part, vec,
+    (grads, weights, wide, tall, stream, normed, rstd, low, turned, prob, ctx, dctx, part, vec,
      w_sem, wide_sem, tall_sem, prob_sem, ctx_sem, turned_sem, end_sem) = rest
     tokens = rows * length
     strips = tokens // STRIP
@@ -734,13 +736,17 @@
     stream_copy = pltpu.make_async_copy(ds_in, stream, end_sem.at[0])
     normed_copy = pltpu.make_async_copy(normed_in, normed, end_sem.at[1])
     rstd_copy = pltpu.make_async_copy(rstd_in, rstd, end_sem.at[2])
-    turned_copy(2, 0).start()
-    wide_copy(act_in, 0).start()
-    stream_copy.start()
+    low_copy = pltpu.make_async_copy(low_in, low, end_sem.at[4])
+    for t in range(PIECES):
+        for source, target, sem in ((turned_in.at[2], turned.at[0], turned_sem), (act_in.at[0], wide.at[0], wide_sem)):
+            at = pl.ds(t * (source.shape[0] // PIECES), source.shape[0] // PIECES)
+            pltpu.make_async_copy(source.at[at], target.at[at], sem.at[0]).start()
     weight_copy(2, 0, 0).start()
+    low_copy.start()
     tall_copy(0).start()
     turned_copy(1, 1).start()
     weight_copy(1, 0, 1).start()
+    stream_copy.start()
     wide_copy(act_in, 1).start()
     tall_copy(1).start()
     weight_copy(2, 1, 2).start()
@@ -789,13 +795,9 @@
 
         @pl.when(j == 0)
         def _():
+            low_copy.wait()
+            turned_copy(1, 1).wait()
             stream_copy.wait()
-
-            @pl.loop(0, strips)
-            def _(s):
-                low[strip(s), :] = stream[strip(s), :].astype(BF)
-
-            turned_copy(1, 1).wait()
 
         weight_copy(2, j, slot).wait()
         tall_copy(j).wait()
@@ -805,12 +807,12 @@
             at = half(n, tokens)
             dactive = mm(low[at, :], weights[slot], NT)
             value = (dactive * tall[parity, at, :].astype(F32)).astype(BF)
-            dexp[at, :] = value
+            tall[2, at, :] = value
             line = pl.ds(10 + z, 1)
             part[line, :] = part[line, :] + jnp.sum(value.astype(F32), axis=0, keepdims=True)
             events("slope", j, n)
 
-        outer(4 + j, 1, dexp[...])
+        outer(4 + j, 1, tall[2])
         events("expand", j)
         emit(4 + j, 1, z)
         weight_copy(1, j, slot + 1).wait()
@@ -818,7 +820,7 @@
         @pl.loop(0, 2)
         def _(n):
             at = half(n, tokens)
-            stream[at, :] = stream[at, :] + mm(dexp[at, :], weights[slot + 1], NT)
+            stream[at, :] = stream[at, :] + mm(tall[2, at, :], weights[slot + 1], NT)
             events("hidden", j, n)
 
         @pl.when(j < 2)
@@ -868,7 +870,7 @@
         @pl.loop(0, 2)
         def _(n):
             at = half(n, tokens)
-            stream[at, :] = stream[at, :] + mm(dproj[j % 2, at, 0 : 3 * width], weights[j, :, 0 : 3 * width], NT)
+            stream[at, :] = stream[at, :] + mm(dproj[j % 3, at, 0 : 3 * width], weights[j, :, 0 : 3 * width], NT)
             events("pull", j, n)
 
     @pl.loop(0, 4)
@@ -905,7 +907,7 @@
             dq = [(mm(part_of(1, h), dscores[h], TN) * HEAD ** (-0.5)).astype(BF) for h in range(heads)]
             dq = [jnp.concatenate(dq, axis=0).T]
             joined = jnp.concatenate(dq + dk + dv, axis=1)
-            dproj[parity, at, 0 : 3 * width] = joined
+            dproj[j % 3, at, 0 : 3 * width] = joined
             line = pl.ds(6 + z, 1)
             before = jnp.where(r == 0, 0.0, part[line, 0 : 3 * width])
             part[line, 0 : 3 * width] = before + jnp.sum(joined.astype(F32), axis=0, keepdims=True)
@@ -916,7 +918,7 @@
                 pl.when(j == k)(lambda k=k: scatter.to_core(2 * k).wait_send())
             pl.when(j == 3)(lambda: scatter.small_stage(part, 0))
 
-        outer(j, 0, dproj[parity, :, 0 : 3 * width])
+        outer(j, 0, dproj[j % 3, :, 0 : 3 * width])
         outer(j, 1, ctx[parity], 3 * width)
         emit(j, 0, z)
         events("project", j)
@@ -925,8 +927,10 @@
         def _():
             wide_copy(qkv_in, j + 2).start()
             ctx_copy(j + 2).start()
-            pull(j)
-
+
+        pl.when(j == 0)(lambda: pull(j))
+
+    pull(1)
     if fused:
         scatter.small_stage(part, 1)
     pull(2)
@@ -962,15 +966,14 @@
     grads, sums, input_grad = pl.pallas_call(
         functools.partial(backward_kernel, fused, rows, length),
         out_shape=(whole_grad, shape((SMALL, D), F32), shape(flat, F32)),
-        in_specs=[vmem] * 2 + [hbm] * 10,
+        in_specs=[vmem] * 2 + [hbm] * 11,
         out_specs=(vmem if fused else hbm, vmem, hbm),
         scratch_shapes=([pltpu.VMEM(s, t) for s, t in Scatter.buffers] + [dma(s) for s in Scatter.sems] if fused else [])
         + [
             pltpu.VMEM((8,) + block, BF),
             pltpu.VMEM((4, D, D), BF),
             pltpu.VMEM((2,) + flat, BF),
-            pltpu.VMEM((2,) + flat, BF),
-            pltpu.VMEM(flat, BF),
+            pltpu.VMEM((3,) + flat, BF),
             pltpu.VMEM(flat, F32),
             pltpu.VMEM(flat, F32),
             pltpu.VMEM((tokens, 128), F32),
@@ -987,7 +990,7 @@
             dma((2,)),
             dma((2,)),
             dma((2,)),
-            dma((4,)),
+            dma((5,)),
         ],
         compiler_params=pltpu.CompilerParams(
             collective_id=1 if fused else None, has_side_effects=True, vmem_limit_bytes=VMEM_MOST
@@ -1006,14 +1009,37 @@
 RATES = (D ** (-0.5), 0.5, (D // 16) ** (-0.5), D ** (-0.5), 0.5, FF ** (-0.5), 0.3)
 
 
+LARGE = (3, 5, 0, 2)
+PIECES = 4
+
+
 def update_kernel(reduced, sums, result_in, input_in, *refs):
-    state, outs, result_out, input_out, result, input_grad, sems = refs[:21], refs[21:49], *refs[49:]
-    moves = [
-        (pltpu.make_async_copy(input_in, input_grad, sems.at[0]), pltpu.make_async_copy(input_grad, input_out, sems.at[1])),
-        (pltpu.make_async_copy(result_in, result, sems.at[2]), pltpu.make_async_copy(result, result_out, sems.at[3])),
-    ]
+    state, outs = list(refs[:21]), list(refs[21:49])
+    result_out, input_out, result, input_grad = refs[49:53]
+    held, load_sem, store_sem, sems = refs[53:81], *refs[81:]
+    piece = input_in.shape[0] // PIECES
+    moves = []
+    for t in range(PIECES):
+        at = pl.ds(t * piece, piece)
+        for j, (source, middle, target) in enumerate(((input_in, input_grad, input_out), (result_in, result, result_out))):
+            moves.append((
+                pltpu.make_async_copy(source.at[at], middle.at[at], sems.at[2 * j, t]),
+                pltpu.make_async_copy(middle.at[at], target.at[at], sems.at[2 * j + 1, t]),
+            ))
+    loads, stores = {}, {}
+    for t, i in enumerate(LARGE):
+        mine = held[7 * t : 7 * t + 7]
+        loads[i] = [pltpu.make_async_copy(state[3 * i + j], mine[j], load_sem.at[t, j]) for j in range(3)]
+        stores[i] = [pltpu.make_async_copy(mine[3 + j], outs[4 * i + j], store_sem.at[t, j]) for j in range(4)]
+        state[3 * i : 3 * i + 3] = mine[:3]
+        outs[4 * i : 4 * i + 4] = mine[3:]
+    for copy in loads[3]:
+        copy.start()
     for load, _ in moves:
         load.start()
+    for i in LARGE[1:]:
+        for copy in loads[i]:
+            copy.start()
     dp, mp = lax.axis_index("dp"), lax.axis_index("mp")
     groups = lax.axis_size("mp")
     width = D // groups
@@ -1024,18 +1050,34 @@
         for j in range(4):
             outs[4 * i + j][at] = new[j]
 
+    def wait(copies):
+        for copy in copies:
+            copy.wait()
+
+    def start(copies):
+        for copy in copies:
+            copy.start()
+
+    wait(loads[3])
     update(3, reduced[1])
+    start(stores[3])
     for load, store in moves:
         load.wait()
         store.start()
+    wait(loads[5])
+    update(5, reduced[2])
+    start(stores[5])
+    wait(loads[0])
     mixing = reduced[0]
     for j in range(3):
         update(0, mixing[:, j * width : (j + 1) * width], j)
+    start(stores[0])
+    wait(loads[2])
     update(2, mixing[:, 3 * width :].T)
-    update(5, reduced[2])
-
-    def lanes(row, count, start):
-        return pltpu.roll(sums[pl.ds(row, count), :], lax.rem(D - start, D), 1)
+    start(stores[2])
+
+    def lanes(row, count, first):
+        return pltpu.roll(sums[pl.ds(row, count), :], lax.rem(D - first, D), 1)
 
     piece = state[3].shape[2]
     moved = lanes(6 + mp, 1, dp * piece)
@@ -1049,6 +1091,8 @@
     update(4, jnp.concatenate(blocks, axis=0).T)
     piece = state[18].shape[1]
     update(6, lanes(0, 8, (dp * groups + mp) * piece)[0:6, 0:piece])
+    for i in LARGE:
+        wait(stores[i])
     for _, store in moves:
         store.wait()
 
@@ -1063,12 +1107,18 @@
     for i in range(7):
         shapes = shapes + [jax.ShapeDtypeStruct(state[3 * i].shape, t) for t in (F32, F32, F32, BF)]
     kept = [jax.ShapeDtypeStruct(a.shape, a.dtype) for a in (result, input_grad)]
+    held = []
+    for i in LARGE:
+        held = held + [pltpu.VMEM(state[3 * i].shape, t) for t in (F32,) * 6 + (BF,)]
+    dma = pltpu.SemaphoreType.DMA
+    state_specs = [hbm if i // 3 in LARGE else vmem for i in range(21)]
+    new_specs = [hbm if i // 4 in LARGE else vmem for i in range(28)]
     *new, result, input_grad = pl.pallas_call(
         update_kernel,
         out_shape=tuple(shapes + kept),
-        in_specs=[vmem] * 2 + [hbm] * 2 + [vmem] * 21,
-        out_specs=(vmem,) * 28 + (hbm,) * 2,
-        scratch_shapes=[pltpu.VMEM(a.shape, a.dtype) for a in kept] + [pltpu.SemaphoreType.DMA((4,))],
+        in_specs=[vmem] * 2 + [hbm] * 2 + state_specs,
+        out_specs=tuple(new_specs) + (hbm,) * 2,
+        scratch_shapes=[pltpu.VMEM(a.shape, a.dtype) for a in kept] + held + [dma((4, 3)), dma((4, 4)), dma((4, PIECES))],
         name="update",
     )(reduced, sums, result, input_grad, *state)
     return result, input_grad, tuple(s.transpose(AXES[i // 4]) for i, s in enumerate(new))

time: 197 us -> 191 us (0.970)
  Pallas kernels: 195 us -> 190 us
    pallas_call x1, Pallas kernels: 87.6 us -> 84.6 us  [run_forward(): pl.pallas_call(functools.partial(forward_kernel, fused, rows, length), ou...]
    pallas_call x1, Pallas kernels: 99.2 us -> 96.3 us  [run_backward(): pl.pallas_call(functools.partial(backward_kernel, fused, rows, length), o...]
where the time goes in v3:
time: 191 us
  Pallas kernels  190 us (99%)
    pallas_call x1, Pallas kernels, run_backward(): pl.pallas_call(functools.partial(backward_kernel, fused, rows, length), o...  96.3 us
    pallas_call x1, Pallas kernels, run_forward(): pl.pallas_call(functools.partial(forward_kernel, fused, rows, length), ou...  84.6 us
    pallas_call x1, Pallas kernels, update_all(): pl.pallas_call(update_kernel, out_shape=tuple(shapes + kept), in_specs=[v...  8.99 us

profile of v3, /device:TPU:0, one launch (start us, length us, event | category | flops | bytes accessed | tf_op | source)
XLA Modules:
  0.0 190.8 jit_solution(9331789639559191863)
XLA Ops:
  0.7 84.6 %forward.1 = (bf16[3,4,4,2,96,768]{5,4,3,2,1,0:T(8,128)(2,1)}, bf16[4,1152,768]{2,1,0:T(8,128)(2,1)}, bf16[4,1152,192]{2,1,0:T(8,128)(2,1)}, bf16[4,4,3,288,288]...) custom-call(bf16[1152,768]{1,0:T(8,128)(2,1)} %bitcast.31, ...), custom_call_target="tpu_custom_call" | custom-call | tf_op jit(solution)/shard_map/forward/pallas_call | solution.py:630
  85.3 96.3 %backward.1 = (f32[3,96,768]{2,1,0:T(8,128)}, f32[16,768]{1,0:T(8,128)}, f32[1152,768]{1,0:T(8,128)}) custom-call(bf16[6,768]{1,0:T(8,128)(2,1)} %refs_0_.2, f32[8,768]{1,0:T(8,128)} %get-tuple-element.76.refs_1_, bf16[3,4,768,768]{3,2,1,0:T(8,128)(2,1)} %bitcast.30, bf16[4,1152,768]{2,1,0:T(8,128)(2,1)} %get-tuple-element.78.refs_3_, ...), custom_call_target="tpu_custom_call" | custom-call | tf_op jit(solution)/shard_map/backward/pallas_call | solution.py:966
  181.6 9.0 %update.1 = (f32[3,96,192]{2,1,0:T(8,128)}, f32[3,96,192]{2,1,0:T(8,128)}, f32[3,96,192]{2,1,0:T(8,128)}, bf16[3,96,192]{2,1,0:T(8,128)(2,1)}, f32[3,2,8]{2,1,0:...) custom-call(f32[3,96,768]{2,1,0:T(8,128)} %get-tuple-element.88.redu, ...), custom_call_target="tpu_custom_call" | custom-call | tf_op jit(solution)/shard_map/update/pallas_call | solution.py:1116

commit v4 on v3

--- a/solution.py
+++ b/solution.py
@@ -354,7 +354,7 @@
      result_out, part_out) = outs
     rest = refs[n_in + 13 :]
     gather_sems, rest = rest[:n_sem], rest[n_sem:]
-    (whole, bias, biases, joint, vec, x, cot, qkv, ctx, prob, act, slope, mixed, normed, rstd, low, turned,
+    (masks, whole, bias, biases, joint, vec, x, cot, qkv, ctx, prob, act, slope, mixed, normed, rstd, low, turned,
      result, part, in_sem, w_sem, qkv_sem, ctx_sem, prob_sem, act_sem, slope_sem, end_sem) = rest
     tokens = rows * length
     strips = tokens // STRIP
@@ -433,6 +433,13 @@
                 for kind, step in due:
                     gather.run(kind, step)
 
+    @pl.loop(0, rows)
+    def _(r):
+        pair = seg_ref[pl.ds(z_own * rows + r, 1), :]
+        number = lax.broadcasted_iota(jnp.int32, (8, length), 0)
+        among = jnp.where(number == pair, 1.0, 0.0).astype(BF)
+        masks[r] = (mm(among, among, TN) - 1.0) * -MASKED
+
     x_copy.wait()
 
     @pl.loop(0, 4)
@@ -458,10 +465,7 @@
         def _(r):
             at = pl.ds(pl.multiple_of(r * length, 32), length)
             pl.when(i >= 1)(lambda: prob_copy(i - 1, r).wait())
-            pair = seg_ref[pl.ds(z_own * rows + r, 1), :]
-            number = lax.broadcasted_iota(jnp.int32, (8, length), 0)
-            among = jnp.where(number == pair, 1.0, 0.0).astype(BF)
-            mask = (mm(among, among, TN) - 1.0) * -MASKED
+            mask = masks[r]
 
             def part_of(j, h):
                 return qkv[slot, at, j * width + h * HEAD : j * width + (h + 1) * HEAD]
@@ -648,6 +652,7 @@
         out_specs=(hbm,) * 13,
         scratch_shapes=([dma(s) for s in Gather.sems] if fused else [])
         + [
+            pltpu.VMEM((rows, length, length), F32),
             pltpu.VMEM((3, 4) + block, BF),
             pltpu.VMEM((VECTORS, D), F32),
             pltpu.VMEM((4, VECTORS, D), F32),

time: 191 us -> 190 us (level)
  no operation moved by 1% of the time
where the time goes in v4:
time: 190 us
  Pallas kernels  189 us (99%)
    pallas_call x1, Pallas kernels, run_backward(): pl.pallas_call(functools.partial(backward_kernel, fused, rows, length), o...  96.3 us
    pallas_call x1, Pallas kernels, run_forward(): pl.pallas_call(functools.partial(forward_kernel, fused, rows, length), ou...  83.8 us
    pallas_call x1, Pallas kernels, update_all(): pl.pallas_call(update_kernel, out_shape=tuple(shapes + kept), in_specs=[v...  8.99 us

profile of v4, /device:TPU:0, one launch (start us, length us, event | category | flops | bytes accessed | tf_op | source)
XLA Modules:
  0.0 190.0 jit_solution(10654123925063966372)
XLA Ops:
  0.7 83.8 %forward.1 = (bf16[3,4,4,2,96,768]{5,4,3,2,1,0:T(8,128)(2,1)}, bf16[4,1152,768]{2,1,0:T(8,128)(2,1)}, bf16[4,1152,192]{2,1,0:T(8,128)(2,1)}, bf16[4,4,3,288,288]...) custom-call(bf16[1152,768]{1,0:T(8,128)(2,1)} %bitcast.31, ...), custom_call_target="tpu_custom_call" | custom-call | tf_op jit(solution)/shard_map/forward/pallas_call | solution.py:634
  84.5 96.3 %backward.1 = (f32[3,96,768]{2,1,0:T(8,128)}, f32[16,768]{1,0:T(8,128)}, f32[1152,768]{1,0:T(8,128)}) custom-call(bf16[6,768]{1,0:T(8,128)(2,1)} %refs_0_.2, f32[8,768]{1,0:T(8,128)} %get-tuple-element.76.refs_1_, bf16[3,4,768,768]{3,2,1,0:T(8,128)(2,1)} %bitcast.30, bf16[4,1152,768]{2,1,0:T(8,128)(2,1)} %get-tuple-element.78.refs_3_, ...), custom_call_target="tpu_custom_call" | custom-call | tf_op jit(solution)/shard_map/backward/pallas_call | solution.py:971
  180.8 9.0 %update.1 = (f32[3,96,192]{2,1,0:T(8,128)}, f32[3,96,192]{2,1,0:T(8,128)}, f32[3,96,192]{2,1,0:T(8,128)}, bf16[3,96,192]{2,1,0:T(8,128)(2,1)}, f32[3,2,8]{2,1,0:...) custom-call(f32[3,96,768]{2,1,0:T(8,128)} %get-tuple-element.88.redu, ...), custom_call_target="tpu_custom_call" | custom-call | tf_op jit(solution)/shard_map/update/pallas_call | solution.py:1121
